TPU v7x, 512 devices: a whole 4x4x16 slice. The times are simulated.
512 devices in a mesh: dp: 64 (over z, x), tm: 8 (over y, core).
Axes of the slice: x: 4, y: 4, z: 16, core: 2. Of those that a mesh axis runs over, the one named last changes fastest.
Arguments:
- mel: bfloat16 [64, 2560, 640], P('dp', 'tm'), may hold values from -6 to 6
- cotangent: bfloat16 [64, 2560, 1024], P('dp', 'tm'), may hold values from -6 to 6
- conv_one: bfloat16 [240, 256], replicated, may hold values from -0.375 to 0.375
- conv_two: bfloat16 [768, 256], replicated, may hold values from -0.21875 to 0.21875
- conv_three: bfloat16 [768, 256], replicated, may hold values from -0.21875 to 0.21875
- linear_weight: bfloat16 [256, 1024], replicated, may hold values from -0.375 to 0.375
- ln_gain: float32 [1024], replicated, may hold values from 0.5 to 1.5
- ln_bias: float32 [1024], replicated, may hold values from -3 to 3
- proj: bfloat16 [1024, 2048], P(None, 'tm'), may hold values from -0.1875 to 0.1875
- dw_kernel: bfloat16 [9, 1024], replicated, may hold values from -2 to 2
- blocks: int32 [64], replicated, may hold values from 1 to 64, as said below
Outputs:
- grad_conv_one: bfloat16 [240, 256], replicated
- grad_conv_two: bfloat16 [768, 256], replicated
- grad_conv_three: bfloat16 [768, 256], replicated
- grad_lin: bfloat16 [256, 1024], replicated
- grad_gain: bfloat16 [1024], replicated
- grad_bias: bfloat16 [1024], replicated
- grad_kernel: bfloat16 [9, 1024], replicated
Inputs may be any that keep to these rules, and one draw needn't show every extreme that they name: blocks sum to 1366 and the largest is exactly 64.
All inputs are finite; a program needn't handle non-finite values.
Results may differ from a plain program's by a relative error of at most 0.017.
Values may be sent and summed in bfloat16 or wider, within the bound.
A program may use at most 64 MiB of HBM per device.

v0:
```python
import jax
import jax.numpy as jnp
from jax import lax
from jax.sharding import PartitionSpec as P

EPSILON = 1e-05


def padded(shard, sides, width):
    for axis, dim in sides:
        devices, length = (lax.axis_size(axis), shard.shape[dim])
        up = [(i, (i + 1) % devices) for i in range(devices - 1)]
        down = [(j, i) for i, j in up]
        last = lax.slice_in_dim(shard, length - width, length, axis=dim)
        leading = lax.slice_in_dim(shard, 0, width, axis=dim)
        before = lax.ppermute(last, axis, up)
        after = lax.ppermute(leading, axis, down)
        shard = jnp.concatenate([before, shard, after], axis=dim)
    return shard


def product(lhs, rhs):
    return jnp.dot(lhs, rhs, preferred_element_type=jnp.float32)


def product_tn(lhs, rhs):
    return lax.dot_general(lhs, rhs, (((0,), (0,)), ((), ())), preferred_element_type=jnp.float32)


def product_nt(lhs, rhs):
    return lax.dot_general(lhs, rhs, (((1,), (1,)), ((), ())), preferred_element_type=jnp.float32)


def make_patches(values, starts):
    last_slot = values[:, -1, :]
    earlier = jnp.concatenate([jnp.zeros_like(last_slot[:1]), last_slot[:-1]], axis=0)
    earlier = earlier * (1 - starts).astype(values.dtype)[:, None]
    before_taps = jnp.concatenate([earlier[:, None, :], values[:, 1:-1:2, :]], axis=1)
    return jnp.concatenate([before_taps, values[:, 0::2, :], values[:, 1::2, :]], axis=2)


def silu_slope(pre_act):
    sigmoid_val = jax.nn.sigmoid(pre_act)
    return sigmoid_val * (1.0 + pre_act * (1.0 - sigmoid_val))


def subsample_forward(mel_rows, starts, conv_one, conv_two, conv_three, linear_weight):
    row_count = mel_rows.shape[0]
    current = mel_rows.reshape(row_count, 8, -1)
    stored = []
    for weight in (conv_one, conv_two, conv_three):
        patches = make_patches(current, starts)
        pre_act = product(patches.reshape(row_count * patches.shape[1], -1), weight)
        stored.append((patches, pre_act))
        current = jax.nn.silu(pre_act).astype(jnp.bfloat16).reshape(row_count, patches.shape[1], -1)
    top_section = current.reshape(row_count, -1)
    hidden = product(top_section, linear_weight).astype(jnp.bfloat16)
    return (hidden, top_section, stored)


def subsample_backward(grad_hidden, top_section, stored, starts, weights, linear_weight):
    row_count = top_section.shape[0]
    grad_lin = product_tn(top_section, grad_hidden)
    grad_act = product_nt(grad_hidden, linear_weight)
    conv_grads = [None, None, None]
    for section_index in (2, 1, 0):
        patches, pre_act = stored[section_index]
        grad_pre = (grad_act.reshape(pre_act.shape) * silu_slope(pre_act)).astype(jnp.bfloat16)
        conv_grads[section_index] = product_tn(patches.reshape(pre_act.shape[0], -1), grad_pre)
        if section_index > 0:
            grad_patch = product_nt(grad_pre, weights[section_index]).reshape(patches.shape)
            input_shape = (row_count, patches.shape[1] * 2, patches.shape[2] // 3)
            _, pullback = jax.vjp(
                lambda inner: make_patches(inner, starts), jnp.zeros(input_shape, jnp.float32)
            )
            grad_act = pullback(grad_patch)[0]
    return (grad_lin, conv_grads)


def gated_forward(hidden, ln_gain, ln_bias, proj):
    values = hidden.astype(jnp.float32)
    centre = jnp.mean(values, axis=-1, keepdims=True)
    spread = jnp.mean(jnp.square(values - centre), axis=-1, keepdims=True)
    inverse_std = lax.rsqrt(spread + EPSILON)
    normed = (values - centre) * inverse_std
    shifted = (normed * ln_gain + ln_bias).astype(jnp.bfloat16)
    projected = product(shifted, proj)
    model_width = proj.shape[0]
    linear_part = projected[:, :model_width]
    sigmoid_gate = jax.nn.sigmoid(projected[:, model_width:])
    gated_rows = (linear_part * sigmoid_gate).astype(jnp.bfloat16)
    return (gated_rows, (normed, inverse_std, linear_part, sigmoid_gate))


def gated_backward(grad_gated, state, ln_gain, proj):
    normed, inverse_std, linear_part, sigmoid_gate = state
    upstream = grad_gated.astype(jnp.float32)
    grad_linear = upstream * sigmoid_gate
    grad_gate = upstream * linear_part * sigmoid_gate * (1.0 - sigmoid_gate)
    grad_projected = jnp.concatenate([grad_linear, grad_gate], axis=-1).astype(jnp.bfloat16)
    grad_shifted = product_nt(grad_projected, proj)
    grad_gain = jnp.sum(grad_shifted * normed, axis=0)
    grad_bias = jnp.sum(grad_shifted, axis=0)
    grad_normed = grad_shifted * ln_gain
    grad_values = inverse_std * (
        grad_normed
        - jnp.mean(grad_normed, axis=-1, keepdims=True)
        - normed * jnp.mean(grad_normed * normed, axis=-1, keepdims=True)
    )
    return (grad_values.astype(jnp.bfloat16), grad_gain, grad_bias)


def owner_tables(blocks, dp_rank, dp_count, total_blocks, work_blocks):
    block_ends = jnp.cumsum(blocks)
    block_starts = block_ends - blocks
    my_blocks = blocks[dp_rank]
    peer_ids = jnp.arange(dp_count, dtype=jnp.int32)
    send_pick = jnp.mod(peer_ids - block_starts[dp_rank], dp_count)
    send_valid = send_pick < my_blocks
    work_rank = jnp.arange(work_blocks, dtype=jnp.int32) * dp_count + dp_rank
    work_valid_mask = work_rank < total_blocks
    work_source = jnp.sum((block_ends[None, :] <= work_rank[:, None]).astype(jnp.int32), axis=1)
    work_source = jnp.minimum(work_source, dp_count - 1)
    return (
        block_starts,
        block_ends,
        send_pick,
        send_valid,
        work_rank,
        work_valid_mask,
        work_source,
    )


def per_device(
    mel,
    cotangent,
    conv_one,
    conv_two,
    conv_three,
    linear_weight,
    ln_gain,
    ln_bias,
    proj,
    dw_kernel,
    blocks,
):
    dp_count = lax.axis_size("dp")
    tm_count = lax.axis_size("tm")
    dp_rank = lax.axis_index("dp")
    tm_rank = lax.axis_index("tm")
    mel_rows = mel[0]
    cot_rows = cotangent[0]
    rows_dev = mel_rows.shape[0]
    block_rows = rows_dev // dp_count
    model_width = linear_weight.shape[1]
    tap_count = dw_kernel.shape[0]
    half_width = tap_count // 2
    rim_rows = half_width + 1
    total_blocks = (dp_count * dp_count + 2) // 3
    work_blocks = (total_blocks + dp_count - 1) // dp_count
    weights = (conv_one, conv_two, conv_three)
    taps_float = dw_kernel.astype(jnp.float32)
    my_blocks = blocks[dp_rank]
    live_rows = my_blocks * block_rows
    row_ids = jnp.arange(rows_dev, dtype=jnp.int32)
    live_mask = row_ids < live_rows
    mel_live = mel_rows * live_mask[:, None].astype(mel_rows.dtype)
    tail_rows = lax.dynamic_slice_in_dim(mel_live, live_rows - rim_rows, rim_rows, 0)
    edge_rows = jnp.concatenate([mel_live[:rim_rows], tail_rows], axis=0)
    edges = padded(edge_rows, (("tm", 0),), rim_rows)
    before_rows = edges[:rim_rows]
    after_rows = edges[3 * rim_rows : 3 * rim_rows + half_width]
    proj_full = lax.all_gather(proj, "tm", axis=1, tiled=True)
    loss_scale = lax.rsqrt(jnp.float32(total_blocks * block_rows * tm_count))
    sequence = jnp.concatenate(
        [before_rows, mel_live, tail_rows[rim_rows - 1 :], after_rows], axis=0
    )
    right_start = rim_rows + rows_dev
    seq_ids = jnp.arange(sequence.shape[0], dtype=jnp.int32)
    starts = ((seq_ids == 0) | (seq_ids == right_start)).astype(jnp.int32)
    hidden, top_section, stored = subsample_forward(
        sequence, starts, conv_one, conv_two, conv_three, linear_weight
    )
    main_hidden = hidden[rim_rows : rim_rows + rows_dev] * live_mask[:, None].astype(jnp.bfloat16)
    side_hidden = jnp.concatenate([hidden[1:rim_rows], hidden[right_start + 1 :]], axis=0)
    side_gated, side_state = gated_forward(side_hidden, ln_gain, ln_bias, proj_full)
    has_left = (tm_rank > 0).astype(jnp.float32)
    has_right = (tm_rank < tm_count - 1).astype(jnp.float32)
    block_starts, block_ends, send_pick, send_valid, work_rank, work_valid_mask, work_source = (
        owner_tables(blocks, dp_rank, dp_count, total_blocks, work_blocks)
    )
    peer_ids = jnp.arange(dp_count, dtype=jnp.int32)
    home_owner = jnp.mod(peer_ids + block_starts[dp_rank], dp_count)
    home_valid = peer_ids < my_blocks
    rank_first = block_starts + jnp.mod(dp_rank - block_starts, dp_count)
    source_valid = rank_first < block_ends
    slot_of = jnp.minimum(rank_first // dp_count, work_blocks - 1)

    def visit(rows, work_fn):
        tiles = rows.reshape(dp_count, block_rows, -1)
        outgoing = tiles[send_pick] * send_valid[:, None, None].astype(rows.dtype)
        incoming = lax.all_to_all(outgoing, "dp", split_axis=0, concat_axis=0, tiled=True)
        gathered = incoming[work_source] * work_valid_mask[:, None, None].astype(rows.dtype)
        result, extra = work_fn(gathered.reshape(work_blocks * block_rows, -1))
        result_tiles = result.reshape(work_blocks, block_rows, -1)
        replies = result_tiles[slot_of] * source_valid[:, None, None].astype(result.dtype)
        returned = lax.all_to_all(replies, "dp", split_axis=0, concat_axis=0, tiled=True)
        placed = returned[home_owner] * home_valid[:, None, None].astype(result.dtype)
        return (placed.reshape(rows_dev, -1), extra)

    def forward_work(rows):
        return gated_forward(rows, ln_gain, ln_bias, proj_full)

    main_gated, main_state = visit(main_hidden, forward_work)
    gated_ext = jnp.concatenate(
        [
            side_gated[:half_width].astype(jnp.float32) * has_left,
            main_gated.astype(jnp.float32),
            jnp.zeros((half_width, model_width), jnp.float32),
        ],
        axis=0,
    )
    gated_ext = lax.dynamic_update_slice_in_dim(
        gated_ext,
        side_gated[half_width:].astype(jnp.float32) * has_right,
        live_rows + half_width,
        0,
    )
    grad_out = cot_rows.astype(jnp.float32) * loss_scale * live_mask[:, None].astype(jnp.float32)
    grad_kernel = jnp.sum(
        jnp.stack(
            [
                grad_out * gated_ext[tap_index : tap_index + rows_dev]
                for tap_index in range(tap_count)
            ],
            axis=0,
        ),
        axis=1,
    )
    ext_rows = rows_dev + 2 * half_width
    grad_padded = jnp.pad(grad_out, ((2 * half_width, 2 * half_width), (0, 0)))
    grad_ext = grad_padded[2 * half_width : 2 * half_width + ext_rows] * taps_float[0]
    for tap_index in range(1, tap_count):
        offset = 2 * half_width - tap_index
        grad_ext = grad_ext + grad_padded[offset : offset + ext_rows] * taps_float[tap_index]
    grad_main = (
        grad_ext[half_width : half_width + rows_dev] * live_mask[:, None].astype(jnp.float32)
    ).astype(jnp.bfloat16)
    grad_side = jnp.concatenate(
        [
            grad_ext[:half_width] * has_left,
            lax.dynamic_slice_in_dim(grad_ext, live_rows + half_width, half_width, 0) * has_right,
        ],
        axis=0,
    ).astype(jnp.bfloat16)
    side_hidden_grad, side_gain, side_bias = gated_backward(
        grad_side, side_state, ln_gain, proj_full
    )

    def backward_work(grads):
        hidden_grad, gain_grad, bias_grad = gated_backward(grads, main_state, ln_gain, proj_full)
        return (hidden_grad, (gain_grad, bias_grad))

    main_hidden_grad, primary_terms = visit(grad_main, backward_work)
    main_hidden_grad = main_hidden_grad * live_mask[:, None].astype(jnp.bfloat16)
    zero_row = jnp.zeros((1, model_width), jnp.bfloat16)
    grad_hidden = jnp.concatenate(
        [
            zero_row,
            side_hidden_grad[:half_width],
            main_hidden_grad,
            zero_row,
            side_hidden_grad[half_width:],
        ],
        axis=0,
    )
    grad_lin, conv_grads = subsample_backward(
        grad_hidden, top_section, stored, starts, weights, linear_weight
    )
    grad_gain = primary_terms[0] + side_gain
    grad_bias = primary_terms[1] + side_bias
    summed = lax.psum(
        (conv_grads[0], conv_grads[1], conv_grads[2], grad_lin, grad_gain, grad_bias, grad_kernel),
        ("dp", "tm"),
    )
    return tuple((piece.astype(jnp.bfloat16) for piece in summed))


def solution(mesh):
    return jax.shard_map(
        per_device,
        mesh=mesh,
        in_specs=(
            P("dp", "tm", None),
            P("dp", "tm", None),
            P(),
            P(),
            P(),
            P(),
            P(),
            P(),
            P(None, "tm"),
            P(),
            P(),
        ),
        out_specs=(P(), P(), P(), P(), P(), P(), P()),
        check_vma=False,
    )
```

profile of v0, /device:TPU:1, one launch (start us, length us, event | category | flops | bytes accessed | tf_op | source)
XLA Modules:
  0.0 576.4 jit_solution(7786700689891024260)
XLA Ops:
  11.5 4.6 collective-permute-start
  16.0 6.1 %collective-permute-start.1 = (bf16[5,640]{0,1:T(8,128)(2,1)S(1)}, bf16[5,640]{0,1:T(8,128)(2,1)}, u32[]{:S(2)}, u32[]{:S(2)}) collective-permute-start(bf16[5,640]{0,1:T(8,128)(2,1)S(1)} %get-tuple-element.42), channel_id=1, source_target_pairs={{1,0},{2,1},{3,2},{4,3},{5,4},{6,5},{7,6},{9,8},{10,9},{11,10},{12... | collective-permute-start | bytes 19208 | tf_op jit(solution)/shard_map/ppermute | solution.py:17
  27.0 1.9 compare_convert_fusion
  28.9 2.2 reshape.360
  31.1 2.9 gather_fusion.2
  43.1 7.7 %slice.193 = bf16[330,2,256]{2,1,0:T(2,128)(2,1)} slice(bf16[330,4,256]{2,1,0:T(4,128)(2,1)S(1)} %reshape.353), slice={[0:330:1], [0:4:2], [0:256:1]} | slice | bytes 675840 | tf_op jit(solution)/shard_map/slice | solution.py:39
  51.8 2.4 slice.194
  58.8 2.6 multiply_convert_fusion.3
  67.2 2.8 gather_fusion
  70.0 2.7 broadcast_multiply_fusion.2
  72.7 68.9 %all_to_all.20 = bf16[64,5,1024]{2,1,0:T(8,128)(2,1)} all-to-all(bf16[64,5,1024]{2,1,0:T(8,128)(2,1)S(1)} %get-tuple-element.65), channel_id=1, replica_groups=mesh['dp'=64,'tm'=8] {'dp'}, dimensions={0} | all-to-all | bytes 1310720 | tf_op jit(solution)/shard_map/all_to_all | solution.py:203
  141.6 5.9 %all-to-all-start = ((bf16[64,5,1024]{2,1,0:T(8,128)(2,1)}), bf16[64,5,1024]{2,1,0:T(8,128)(2,1)}, u32[]{:S(2)}, u32[]{:S(2)}) async-start(bf16[64,5,1024]{2,1,0:T(8,128)(2,1)} %get-tuple-element.66), calls=%async_computation | async-start | bytes 2097152 | tf_op jit(solution)/shard_map/all_to_all | solution.py:203
  148.0 1.8 gather_fusion.3
  150.0 51.4 %all-to-all-done = bf16[64,5,1024]{2,1,0:T(8,128)(2,1)} async-done(((bf16[64,5,1024]{2,1,0:T(8,128)(2,1)}), bf16[64,5,1024]{2,1,0:T(8,128)(2,1)}, u32[]{:S(2)}, u32[]{:S(2)}) %all-to-all-start) | async-done | bytes 655392 | tf_op jit(solution)/shard_map/all_to_all | solution.py:203
  201.4 1.8 gather_fusion.1
  204.2 3.2 fusion.36
  208.3 2.1 multiply_reduce_fusion
  215.1 3.1 broadcast_multiply_fusion
  218.1 7.1 %all-to-all-start.3 = ((bf16[64,5,1024]{2,1,0:T(8,128)(2,1)}), bf16[64,5,1024]{2,1,0:T(8,128)(2,1)}, u32[]{:S(2)}, u32[]{:S(2)}) async-start(bf16[64,5,1024]{2,1,0:T(8,128)(2,1)} %get-tuple-element.63), calls=%async_computation.3 | async-start | bytes 2097152 | tf_op jit(solution)/shard_map/all_to_all | solution.py:208
  226.9 49.2 %all-to-all-done.3 = bf16[64,5,1024]{2,1,0:T(8,128)(2,1)} async-done(((bf16[64,5,1024]{2,1,0:T(8,128)(2,1)}), bf16[64,5,1024]{2,1,0:T(8,128)(2,1)}, u32[]{:S(2)}, u32[]{:S(2)}) %all-to-all-start.3) | async-done | bytes 655392 | tf_op jit(solution)/shard_map/all_to_all | solution.py:208
  276.2 9.1 %all-to-all-start.2 = ((bf16[64,5,1024]{2,1,0:T(8,128)(2,1)}), bf16[64,5,1024]{2,1,0:T(8,128)(2,1)S(1)}, u32[]{:S(2)}, u32[]{:S(2)}) async-start(bf16[64,5,1024]{2,1,0:T(8,128)(2,1)} %get-tuple-element.64), calls=%async_computation.2 | async-start | bytes 2097152 | tf_op jit(solution)/shard_map/all_to_all | solution.py:208
  286.4 3.0 fusion.70
  293.1 1.8 gather_fusion.7
  296.1 40.6 %all-to-all-done.2 = bf16[64,5,1024]{2,1,0:T(8,128)(2,1)S(1)} async-done(((bf16[64,5,1024]{2,1,0:T(8,128)(2,1)}), bf16[64,5,1024]{2,1,0:T(8,128)(2,1)S(1)}, u32[]{:S(2)}, u32[]{:S(2)}) %all-to-all-start.2) | async-done | bytes 655392 | tf_op jit(solution)/shard_map/all_to_all | solution.py:208
  338.4 2.3 multiply_convert_fusion.5
  349.9 2.5 reshape.364
  352.5 2.0 fusion.99
  354.5 2.6 fusion.98
  359.4 2.2 pad.39
  365.7 2.6 fusion.24
  381.3 5.5 reduce_sum.153
  386.8 182.5 %all-reduce.15 = (bf16[240,256]{1,0:T(8,128)(2,1)}, bf16[768,256]{1,0:T(8,128)(2,1)}, bf16[768,256]{1,0:T(8,128)(2,1)}, bf16[256,1024]{1,0:T(8,128)(2,1)}, bf16[...) all-reduce(f32[240,256]{1,0:T(8,128)S(1)} %fusion.24, ...), channel_id=1, replica_groups=mesh['dp'=64,'tm'=8] {'dp','tm'}, use_global_device_ids=true, to_apply=%region_10.11 | all-reduce | flops 728064 | bytes 4368384 | tf_op jit(solution)/shard_map/psum | solution.py:283
  (227 shorter events, 73.2 us)
Async XLA Ops:
  7.2 57.3 %copy-start = (bf16[256,1024]{1,0:T(8,128)(2,1)S(1)}, bf16[256,1024]{1,0:T(8,128)(2,1)}, u32[]{:S(2)}) copy-start(bf16[256,1024]{1,0:T(8,128)(2,1)} %param.16) | copy-start | bytes 1572868
  7.2 197.0 %all-gather.2.cloned.1.call-start = ((), (), s32[]{:S(2)}) async-start(), calls=%async_computation.4 | async-start | bytes 4718592 | tf_op jit(solution)/shard_map/all_gather | solution.py:174
  7.9 14.3 %copy-start.34 = (s32[64]{0:T(128)S(1)}, s32[64]{0:T(128)}, u32[]{:S(2)}) copy-start(s32[64]{0:T(128)} %param.21) | copy-start | bytes 772
  9.9 14.4 %copy-start.26 = (bf16[9,1024]{1,0:T(8,128)(2,1)S(1)}, bf16[9,1024]{1,0:T(8,128)(2,1)}, u32[]{:S(2)}) copy-start(bf16[9,1024]{1,0:T(8,128)(2,1)} %param.20) | copy-start | bytes 55300
  9.9 14.6 %copy-start.2 = (bf16[1,320,1024]{2,1,0:T(8,128)(2,1)S(1)}, bf16[1,320,1024]{2,1,0:T(8,128)(2,1)}, u32[]{:S(2)}) copy-start(bf16[1,320,1024]{2,1,0:T(8,128)(2,1)} %param.12) | copy-start | bytes 1966084
  11.5 22.5 %collective-permute-start = (bf16[5,640]{0,1:T(8,128)(2,1)S(1)}, bf16[5,640]{0,1:T(8,128)(2,1)}, u32[]{:S(2)}, u32[]{:S(2)}) collective-permute-start(bf16[5,640]{0,1:T(8,128)(2,1)S(1)} %get-tuple-element.41), channel_id=1, source_target_pairs={{0,1},{1,2},{2,3},{3,4},{4,5},{5,6},{6,7},{8,9},{9,10},{10,11},{11... | collective-permute-start | bytes 19208 | tf_op jit(solution)/shard_map/ppermute | solution.py:16
  16.0 17.9 %collective-permute-start.1 = (bf16[5,640]{0,1:T(8,128)(2,1)S(1)}, bf16[5,640]{0,1:T(8,128)(2,1)}, u32[]{:S(2)}, u32[]{:S(2)}) collective-permute-start(bf16[5,640]{0,1:T(8,128)(2,1)S(1)} %get-tuple-element.42), channel_id=1, source_target_pairs={{1,0},{2,1},{3,2},{4,3},{5,4},{6,5},{7,6},{9,8},{10,9},{11,10},{12... | collective-permute-start | bytes 19208 | tf_op jit(solution)/shard_map/ppermute | solution.py:17
  22.2 2.5 copy-start.17
  22.5 3.5 copy-start.36
  35.6 3.0 copy-start.40
  54.2 2.2 copy-start.7
  62.5 2.3 copy-start.19
  141.6 6.2 %copy-start.37 = (s32[64]{0:T(128)S(1)}, s32[64]{0:T(128)}, u32[]{:S(2)}) copy-start(s32[64]{0:T(128)} %copy-done.36) | copy-start | bytes 772
  141.6 6.4 %copy-start.39 = (s32[64]{0:T(128)S(1)}, s32[64]{0:T(128)}, u32[]{:S(2)}) copy-start(s32[64]{0:T(128)} %get-tuple-element.23) | copy-start | bytes 772
  141.6 59.8 %all-to-all-start = ((bf16[64,5,1024]{2,1,0:T(8,128)(2,1)}), bf16[64,5,1024]{2,1,0:T(8,128)(2,1)}, u32[]{:S(2)}, u32[]{:S(2)}) async-start(bf16[64,5,1024]{2,1,0:T(8,128)(2,1)} %get-tuple-element.66), calls=%async_computation | async-start | bytes 2097152 | tf_op jit(solution)/shard_map/all_to_all | solution.py:203
  149.8 54.3 %copy-start.23 = (f32[1024]{0:T(1024)S(1)}, f32[1024]{0:T(1024)}, u32[]{:S(2)}) copy-start(f32[1024]{0:T(1024)} %param.17) | copy-start | bytes 12292
  149.8 54.3 %copy-start.29 = (f32[1024]{0:T(1024)S(1)}, f32[1024]{0:T(1024)}, u32[]{:S(2)}) copy-start(f32[1024]{0:T(1024)} %param.18) | copy-start | bytes 12292
  204.2 4.1 copy-start.3
  218.1 7.2 %copy-start.38 = (bf16[64]{0:T(256)(128)(2,1)S(1)}, bf16[64]{0:T(256)(128)(2,1)}, u32[]{:S(2)}) copy-start(bf16[64]{0:T(256)(128)(2,1)} %get-tuple-element.73) | copy-start | bytes 388
  218.1 58.0 %all-to-all-start.3 = ((bf16[64,5,1024]{2,1,0:T(8,128)(2,1)}), bf16[64,5,1024]{2,1,0:T(8,128)(2,1)}, u32[]{:S(2)}, u32[]{:S(2)}) async-start(bf16[64,5,1024]{2,1,0:T(8,128)(2,1)} %get-tuple-element.63), calls=%async_computation.3 | async-start | bytes 2097152 | tf_op jit(solution)/shard_map/all_to_all | solution.py:208
  225.3 120.2 %copy-start.27 = (f32[329]{0:T(512)}, f32[329]{0:T(512)S(1)}, u32[]{:S(2)}) copy-start(f32[329]{0:T(512)S(1)} %slice.283) | copy-start | bytes 3952
  276.2 60.5 %all-to-all-start.2 = ((bf16[64,5,1024]{2,1,0:T(8,128)(2,1)}), bf16[64,5,1024]{2,1,0:T(8,128)(2,1)S(1)}, u32[]{:S(2)}, u32[]{:S(2)}) async-start(bf16[64,5,1024]{2,1,0:T(8,128)(2,1)} %get-tuple-element.64), calls=%async_computation.2 | async-start | bytes 2097152 | tf_op jit(solution)/shard_map/all_to_all | solution.py:208
  286.4 3.5 copy-start.4
  354.4 2.7 copy-start.28
  365.7 2.6 copy-start.5
  365.7 2.6 copy-start.24
  365.7 2.6 copy-start.32
  381.2 5.6 copy-start.8
  381.2 5.6 copy-start.10
  381.2 5.6 copy-start.30
  381.2 5.6 copy-start.31
  381.2 188.1 %copy-start.1 = (bf16[256,1024]{1,0:T(8,128)(2,1)S(1)}, bf16[256,1024]{1,0:T(8,128)(2,1)}, u32[]{:S(2)}) copy-start(bf16[256,1024]{1,0:T(8,128)(2,1)} %param.16) | copy-start | bytes 1572868
  (17 other events, 21.0 us)
Sparse Core Ops, SparseCore 0:
  10.1 48.9 all-gather.1
where the time goes:
time: 587 us; the launch traced here: 576 us
  blocking collectives  251 us (43%)
  waiting for transfers between devices  142 us (24%)
  local copies, waits for them, and re-layouts  69.6 us (12%)
  other arithmetic  41.9 us (7%)
  starting transfers between devices  32.9 us (6%)
  matrix products  22.6 us (4%)
  between operations  16 us (3%)
    psum x1, blocking collectives, per_device(): lax.psum((conv_grads[0], conv_grads[1], conv_grads[2], grad_lin, grad_gai...  182 us
    all_to_all x2, waiting for transfers between devices, visit(): lax.all_to_all(replies, 'dp', split_axis=0, concat_axis=0, tiled=True)  89.8 us
    all_to_all x1, blocking collectives, visit(): lax.all_to_all(outgoing, 'dp', split_axis=0, concat_axis=0, tiled=True)  68.9 us
    all_to_all x1, waiting for transfers between devices, visit(): lax.all_to_all(outgoing, 'dp', split_axis=0, concat_axis=0, tiled=True)  51.4 us
    all_to_all x2, starting transfers between devices, visit(): lax.all_to_all(replies, 'dp', split_axis=0, concat_axis=0, tiled=True)  16.2 us
  transfers between devices with their start and end apart: 6, of which 3 were waited for; matrix products, arithmetic and copies ran while one was open for 12% of the time, Pallas kernels for 0%

commit v1 on v0

v1 whole, which is shorter than its diff:
```python
import jax
import jax.numpy as jnp
from jax import lax
from jax.sharding import PartitionSpec as P

EPSILON = 1e-05
BF = jnp.bfloat16
F32 = jnp.float32


def mm(lhs, rhs):
    return jnp.dot(lhs, rhs, preferred_element_type=F32)


def mm_tn(lhs, rhs):
    return lax.dot_general(lhs, rhs, (((0,), (0,)), ((), ())), preferred_element_type=F32)


def mm_nt(lhs, rhs):
    return lax.dot_general(lhs, rhs, (((1,), (1,)), ((), ())), preferred_element_type=F32)


def roll(values, shift):
    return jnp.roll(values, shift, axis=0)


def silu(z):
    return (z * jax.nn.sigmoid(z)).astype(BF)


def through_silu(grad, z):
    s = jax.nn.sigmoid(z)
    return (grad * (s * (1.0 + z * (1.0 - s)))).astype(BF)


def wide_conv_one(conv):
    bins = conv.shape[0] // 3
    columns = []
    for slot in range(4):
        if slot == 0:
            column = jnp.concatenate(
                [conv[bins:], jnp.zeros((6 * bins, conv.shape[1]), conv.dtype), conv[:bins]], axis=0
            )
        else:
            top = (2 * slot - 1) * bins
            column = jnp.pad(conv, ((top, 9 * bins - top - 3 * bins), (0, 0)))
        columns.append(column)
    return jnp.concatenate(columns, axis=1)


def narrow_conv_one(wide):
    bins = wide.shape[0] // 9
    ch = wide.shape[1] // 4
    total = jnp.concatenate([wide[8 * bins :, :ch], wide[: 2 * bins, :ch]], axis=0)
    for slot in range(1, 4):
        top = (2 * slot - 1) * bins
        total = total + wide[top : top + 3 * bins, slot * ch : (slot + 1) * ch]
    return total


def per_device(
    mel,
    cotangent,
    conv_one,
    conv_two,
    conv_three,
    linear_weight,
    ln_gain,
    ln_bias,
    proj,
    dw_kernel,
    blocks,
):
    tm_count = lax.axis_size("tm")
    tm_rank = lax.axis_index("tm")
    dp_count = lax.axis_size("dp")
    rows_dev = mel.shape[1]
    bins = conv_one.shape[0] // 3
    ch = conv_two.shape[1]
    width = linear_weight.shape[1]
    taps = dw_kernel.shape[0]
    half = taps // 2
    rows = rows_dev + 16
    total_blocks = (dp_count * dp_count + 2) // 3
    block_rows = rows_dev // dp_count
    live = blocks[lax.axis_index("dp")] * block_rows
    scale = lax.rsqrt(F32(total_blocks * block_rows * tm_count))

    proj_full = lax.all_gather(proj, "tm", axis=1, tiled=True)
    up = [(i, i + 1) for i in range(tm_count - 1)]
    down = [(i + 1, i) for i in range(tm_count - 1)]
    tail = lax.dynamic_slice_in_dim(mel[0], live - half - 1, half + 1, 0)
    before = lax.ppermute(tail, "tm", up)
    after = lax.ppermute(mel[0, :half], "tm", down)
    ids = jnp.arange(rows, dtype=jnp.int32)[:, None]
    own = ids < live
    x = jnp.where(own, jnp.pad(mel[0], ((0, rows - rows_dev), (0, 0))), jnp.zeros((), BF))
    x = lax.dynamic_update_slice(x, after, (live, 0))
    x = lax.dynamic_update_slice(x, before, (rows - half - 1, 0))
    valid = (
        own
        | ((ids < live + half) & (tm_rank < tm_count - 1))
        | ((ids >= rows - half) & (tm_rank > 0))
    )
    cot = jnp.where(own, jnp.pad(cotangent[0], ((0, rows - rows_dev), (0, 0))), jnp.zeros((), BF))

    x_wide = jnp.concatenate([x, roll(x[:, 7 * bins :], 1)], axis=1)
    w_one = wide_conv_one(conv_one)
    z1 = mm(x_wide, w_one)
    a1 = silu(z1)
    z2 = jnp.concatenate(
        [
            mm(a1[:, : 2 * ch], conv_two[ch:]) + mm(roll(a1[:, 3 * ch :], 1), conv_two[:ch]),
            mm(a1[:, ch:], conv_two),
        ],
        axis=1,
    )
    a2 = silu(z2)
    z3 = mm(a2, conv_three[ch:]) + mm(roll(a2[:, ch:], 1), conv_three[:ch])
    a3 = silu(z3)
    h = mm(a3, linear_weight).astype(BF).astype(F32)
    centred = h - jnp.mean(h, axis=-1, keepdims=True)
    inverse = lax.rsqrt(jnp.mean(jnp.square(centred), axis=-1, keepdims=True) + EPSILON)
    n = centred * inverse
    u = (n * ln_gain + ln_bias).astype(BF)
    m = mm(u, proj_full)
    value = m[:, :width]
    gate = jax.nn.sigmoid(m[:, width:])
    gated = jnp.where(valid, (value * gate).astype(BF).astype(F32), 0.0)

    c = cot.astype(F32) * scale
    kernel_float = dw_kernel.astype(F32)
    grad_kernel = []
    eg = jnp.zeros((rows, width), F32)
    for k in range(taps):
        grad_kernel.append(jnp.sum(c * roll(gated, half - k), axis=0))
        eg = eg + roll(c, k - half) * kernel_float[k]
    grad_kernel = jnp.stack(grad_kernel, axis=0)
    eg = jnp.where(valid, eg, 0.0).astype(BF).astype(F32)

    value_grad = eg * gate
    gate_grad = value_grad * value * (1.0 - gate)
    em = jnp.concatenate([value_grad, gate_grad], axis=1).astype(BF)
    du = mm_nt(em, proj_full)
    grad_gain = jnp.sum(du * n, axis=0)
    grad_bias = jnp.sum(du, axis=0)
    e = du * ln_gain
    dh = (
        inverse
        * (e - jnp.mean(e, axis=-1, keepdims=True) - n * jnp.mean(e * n, axis=-1, keepdims=True))
    ).astype(BF)
    grad_lin = mm_tn(a3, dh)
    ez3 = through_silu(mm_nt(dh, linear_weight), z3)
    ez3_next = roll(ez3, -1)
    grad_three = jnp.concatenate([mm_tn(a2[:, ch:], ez3_next), mm_tn(a2, ez3)], axis=0)
    da2 = mm_nt(ez3, conv_three[ch:])
    da2 = jnp.concatenate([da2[:, :ch], da2[:, ch:] + mm_nt(ez3_next, conv_three[:ch])], axis=1)
    ez2 = through_silu(da2, z2)
    first, second = ez2[:, :ch], ez2[:, ch:]
    first_next = roll(first, -1)
    grad_two = (
        jnp.concatenate([mm_tn(a1[:, 3 * ch :], first_next), mm_tn(a1[:, : 2 * ch], first)], axis=0)
        + mm_tn(a1[:, ch:], second)
    )
    left = mm_nt(first, conv_two[ch:])
    right = mm_nt(second, conv_two)
    over = mm_nt(first_next, conv_two[:ch])
    da1 = jnp.concatenate(
        [left[:, :ch], left[:, ch:] + right[:, :ch], right[:, ch : 2 * ch], right[:, 2 * ch :] + over],
        axis=1,
    )
    ez1 = through_silu(da1, z1)
    grad_one = narrow_conv_one(mm_tn(x_wide, ez1))
    summed = lax.psum(
        (grad_one, grad_two, grad_three, grad_lin, grad_gain, grad_bias, grad_kernel), ("dp", "tm")
    )
    return tuple(piece.astype(BF) for piece in summed)


def solution(mesh):
    return jax.shard_map(
        per_device,
        mesh=mesh,
        in_specs=(
            P("dp", "tm", None),
            P("dp", "tm", None),
            P(),
            P(),
            P(),
            P(),
            P(),
            P(),
            P(None, "tm"),
            P(),
            P(),
        ),
        out_specs=(P(), P(), P(), P(), P(), P(), P()),
        check_vma=False,
    )
```

time: 587 us -> 279 us (0.48); the launches traced: 576 us -> 278 us
  waiting for transfers between devices: 142 us -> 22.4 us
  blocking collectives: 251 us -> 182 us
  local copies, waits for them, and re-layouts: 69.6 us -> 18.1 us
  other arithmetic: 41.9 us -> 13.7 us
  starting transfers between devices: 32.9 us -> 10.7 us
  matrix products: 22.6 us -> 15.8 us
    all_to_all x3 -> x0, waiting for transfers between devices: 141 us -> none  [the longest x2 89.8 us: visit(): lax.all_to_all(replies, 'dp', split_axis=0, concat_axis=0, tiled=True)]
    all_to_all x1 -> x0, blocking collectives: 68.9 us -> none  [visit(): lax.all_to_all(outgoing, 'dp', split_axis=0, concat_axis=0, tiled=True)]
    all_to_all x3 -> x0, starting transfers between devices: 22.1 us -> none  [the longest x2 16.2 us: visit(): lax.all_to_all(replies, 'dp', split_axis=0, concat_axis=0, tiled=True)]
    all_gather x1, waiting for transfers between devices: 0.02 us -> 21.7 us  [per_device(): proj_full = lax.all_gather(proj, 'tm', axis=1, tiled=True)]
    gather x12 -> x0, local copies, waits for them, and re-layouts: 17.4 us -> none  [the longest x2 5.68 us: visit(): outgoing = tiles[send_pick] * send_valid[:, None, None].astype(rows.dtype)]
    reshape x11 -> x0, local copies, waits for them, and re-layouts: 13.8 us -> none  [the longest x2 3.46 us: visit(): tiles = rows.reshape(dp_count, block_rows, -1)]
    unnamed x8 -> x0, other arithmetic: 10.7 us -> none
    dot_general x15 -> x22, matrix products: 22.6 us -> 15.8 us  [the longest x8 7.77 us: mm(): return jnp.dot(lhs, rhs, preferred_element_type=F32)]
  transfers between devices with their start and end apart: 6 -> 3, of which waited for: 3 -> 1; matrix products, arithmetic and copies ran while one was open for 12% -> 6% of each run, Pallas kernels for 0% -> 0%
where the time goes in v1:
time: 279 us; the launch traced here: 278 us
  blocking collectives  182 us (65%)
  waiting for transfers between devices  22.4 us (8%)
  local copies, waits for them, and re-layouts  18.1 us (6%)
  matrix products  15.8 us (6%)
  between operations  15.5 us (6%)
  other arithmetic  13.7 us (5%)
  starting transfers between devices  10.7 us (4%)
    psum x1, blocking collectives, per_device(): lax.psum((grad_one, grad_two, grad_three, grad_lin, grad_gain, grad_bias,...  182 us
    all_gather x1, waiting for transfers between devices, per_device(): proj_full = lax.all_gather(proj, 'tm', axis=1, tiled=True)  21.7 us
    ppermute x1, starting transfers between devices, per_device(): after = lax.ppermute(mel[0, :half], 'tm', down)  8.73 us
    slice x26, local copies, waits for them, and re-layouts, roll(): return jnp.roll(values, shift, axis=0)  8.49 us
    dot_general x8, matrix products, mm(): return jnp.dot(lhs, rhs, preferred_element_type=F32)  7.77 us
    unnamed x62, local copies, waits for them, and re-layouts  6.41 us
  transfers between devices with their start and end apart: 3, of which 1 were waited for; matrix products, arithmetic and copies ran while one was open for 6% of the time, Pallas kernels for 0%

profile of v1, /device:TPU:1, one launch (start us, length us, event | category | flops | bytes accessed | tf_op | source)
XLA Modules:
  0.0 278.0 jit_solution(4416962961547621264)
XLA Ops:
  7.3 0.7 all-gather.2.cloned.1.call-update
  7.9 0.7 slice_bitcast_fusion
  8.6 8.7 %collective-permute-start = (bf16[4,640]{1,0:T(4,128)(2,1)S(1)}, bf16[4,640]{1,0:T(4,128)(2,1)S(1)}, u32[]{:S(2)}, u32[]{:S(2)}) collective-permute-start(bf16[4,640]{1,0:T(4,128)(2,1)S(1)} %slice_bitcast_fusion), channel_id=1, source_target_pairs={{1,0},{2,1},{3,2},{4,3},{5,4},{6,5},{7,6},{9,8},{10,9},{11,10},{12... | collective-permute-start | bytes 15368 | tf_op jit(solution)/shard_map/ppermute | solution.py:94
  17.4 1.2 dynamic_slice.8
  19.3 0.7 dynamic-slice_bitcast_fusion
  20.0 1.9 collective-permute-start.1
  22.0 0.8 convert_element_type.86
  22.8 1.3 convert_multiply_fusion.1
  24.3 1.3 fusion.153
  25.6 1.9 fusion.151
  27.5 1.9 fusion.149
  29.4 1.8 fusion.147
  31.9 1.9 multiply_convert_fusion.2
  34.8 0.6 copy-done.18
  35.9 0.5 convert_reduce_fusion
  36.7 0.5 copy-done.16
  37.3 21.7 %all-gather.2.cloned.1.call-done = bf16[1024,2048]{1,0:T(8,128)(2,1)} async-done(((bf16[1024,256]{1,0:T(8,128)(2,1)}), bf16[1024,2048]{1,0:T(8,128)(2,1)}) %all-gather.2.cloned.1.call-update) | async-done | bytes 4194320 | tf_op jit(solution)/shard_map/all_gather | solution.py:89
  59.1 4.2 %fusion.76 = f32[336,2048]{1,0:T(8,128)S(1)} fusion(bf16[1024,2048]{1,0:T(8,128)(2,1)} %all-gather.2.cloned.1.call-done, bf16[336,1024]{1,0:T(8,128)(2,1)} %copy-done.16, f32[1024]{0:T(1024)S(1)} %copy-done.29, f32[1024]{0:T(1024)S(1)} %copy-done.27, f32[336]{0:T(512)S(1)} %add_rsqrt_fusion, f32[336]{0:T(512)S(1)} %broadcast_multiply_fusion.2), kind=kOutput, calls=%fused_computation.107 | convolution fusion | flops 1411350528 | bytes 7645824 | tf_op jit(solution)/shard_map/dot_general | solution.py:12
  64.3 5.0 %fusion.73 = (bf16[336,1024]{1,0:T(8,128)(2,1)S(1)}, bf16[336,1024]{1,0:T(8,128)(2,1)S(1)}) fusion(f32[336,2048]{1,0:T(8,128)S(1)} %fusion.76, f32[1024]{0:T(1024)S(1)} %bitcast.49, f32[332,1024]{1,0:T(8,128)S(1)} %copy-done.9, f32[4,1024]{1,0:T(4,128)S(1)} %get-tuple-element.50, f32[1024]{0:T(1024)S(1)} %bitcast.48, f32[333,1024]{1,0:T(8,128)S(1)} %copy-done.7, ...), kind=kLoop, calls=%fused_computation.93 | loop fusion | flops 12042240 | bytes 14455456 | tf_op jit(solution)/shard_map/convert
  69.2 0.6 convert_select_fusion
  70.3 1.3 copy-done.28
  71.6 2.0 fusion.44
  73.7 0.5 fusion.43
  74.1 0.5 copy-done.24
  75.0 1.5 fusion.137
  80.5 0.9 copy-done.21
  81.4 0.5 copy-done.30
  81.9 1.1 fusion.83
  84.4 0.4 convolution_add_fusion
  84.9 1.0 fusion.48
  85.9 3.4 %fusion.54 = (f32[1024]{0:T(1024)S(1)}, f32[1024]{0:T(1024)S(1)}, f32[1024]{0:T(1024)S(1)}, f32[1024]{0:T(1024)S(1)}, f32[1024]{0:T(1024)S(1)}, /*index=5*/f32[1024]{0:T(1024)S(1)}) fusion(f32[4,1024]{1,0:T(4,128)S(1)} %get-tuple-element.45, f32[332,1024]{1,0:T(8,128)S(1)} %get-tuple-element.43, bf16[320,1024]{1,0:T(8,128)(2,1)S(1)} %bitcast.40, ...), kind=kLoop, calls=%fused_computation.60 | loop fusion | flops 6875136 | bytes 8937808 | tf_op jit(solution)/shard_map/reduce_sum | solution.py:136
  89.4 181.8 %all-reduce.7 = (bf16[240,256]{1,0:T(8,128)(2,1)}, bf16[768,256]{1,0:T(8,128)(2,1)}, bf16[768,256]{1,0:T(8,128)(2,1)}, bf16[256,1024]{1,0:T(8,128)(2,1)}, bf16[1...) all-reduce(f32[240,256]{1,0:T(8,128)S(1)} %slice_add_fusion.1, ...), channel_id=1, replica_groups=mesh['dp'=64,'tm'=8] {'dp','tm'}, use_global_device_ids=true, to_apply=%region_4.5 | all-reduce | flops 728064 | bytes 4368384 | tf_op jit(solution)/shard_map/psum | solution.py:174
  (121 shorter events, 9.7 us)
Async XLA Ops:
  7.2 28.7 %copy-start = (bf16[256,1024]{1,0:T(8,128)(2,1)S(1)}, bf16[256,1024]{1,0:T(8,128)(2,1)}, u32[]{:S(2)}) copy-start(bf16[256,1024]{1,0:T(8,128)(2,1)} %param.16) | copy-start | bytes 1572868
  7.2 17.0 %copy-start.22 = (bf16[1,320,640]{2,1,0:T(8,128)(2,1)S(1)}, bf16[1,320,640]{2,1,0:T(8,128)(2,1)}, u32[]{:S(2)}) copy-start(bf16[1,320,640]{2,1,0:T(8,128)(2,1)} %param.11) | copy-start | bytes 1228804
  7.2 16.9 %copy-start.25 = (bf16[9,1024]{1,0:T(8,128)(2,1)S(1)}, bf16[9,1024]{1,0:T(8,128)(2,1)}, u32[]{:S(2)}) copy-start(bf16[9,1024]{1,0:T(8,128)(2,1)} %param.20) | copy-start | bytes 55300
  7.2 51.8 %all-gather.2.cloned.1.call-start = ((), (), s32[]{:S(2)}) async-start(), calls=%async_computation | async-start | bytes 4718592 | tf_op jit(solution)/shard_map/all_gather | solution.py:89
  8.6 22.6 %collective-permute-start = (bf16[4,640]{1,0:T(4,128)(2,1)S(1)}, bf16[4,640]{1,0:T(4,128)(2,1)S(1)}, u32[]{:S(2)}, u32[]{:S(2)}) collective-permute-start(bf16[4,640]{1,0:T(4,128)(2,1)S(1)} %slice_bitcast_fusion), channel_id=1, source_target_pairs={{1,0},{2,1},{3,2},{4,3},{5,4},{6,5},{7,6},{9,8},{10,9},{11,10},{12... | collective-permute-start | bytes 15368 | tf_op jit(solution)/shard_map/ppermute | solution.py:94
  20.0 11.4 %collective-permute-start.1 = (bf16[5,640]{1,0:T(8,128)(2,1)S(1)}, bf16[5,640]{1,0:T(8,128)(2,1)S(1)}, u32[]{:S(2)}, u32[]{:S(2)}) collective-permute-start(bf16[5,640]{1,0:T(8,128)(2,1)S(1)} %dynamic-slice_bitcast_fusion), channel_id=1, source_target_pairs={{0,1},{1,2},{2,3},{3,4},{4,5},{5,6},{6,7},{8,9},{9,10},{10,11},{11... | collective-permute-start | bytes 19208 | tf_op jit(solution)/shard_map/ppermute | solution.py:93
  29.4 2.4 copy-start.26
  29.4 2.4 slice-start
  29.4 2.4 slice-start.1
  31.6 2.1 copy-start.20
  31.9 1.9 copy-start.2
  34.3 1.4 copy-start.12
  34.3 1.1 copy-start.18
  34.6 1.3 copy-start.14
  35.9 23.1 %copy-start.27 = (f32[1024]{0:T(1024)S(1)}, f32[1024]{0:T(1024)}, u32[]{:S(2)}) copy-start(f32[1024]{0:T(1024)} %param.17) | copy-start | bytes 12292
  35.9 23.1 %copy-start.29 = (f32[1024]{0:T(1024)S(1)}, f32[1024]{0:T(1024)}, u32[]{:S(2)}) copy-start(f32[1024]{0:T(1024)} %param.18) | copy-start | bytes 12292
  37.3 26.1 %copy-start.1 = (bf16[1,320,1024]{2,1,0:T(8,128)(2,1)S(1)}, bf16[1,320,1024]{2,1,0:T(8,128)(2,1)}, u32[]{:S(2)}) copy-start(bf16[1,320,1024]{2,1,0:T(8,128)(2,1)} %param.12) | copy-start | bytes 1966084
  59.0 4.3 %copy-start.3 = (f32[335,1024]{1,0:T(8,128)S(1)}, f32[335,1024]{1,0:T(8,128)}, u32[]{:S(2)}) copy-start(f32[335,1024]{1,0:T(8,128)} %get-tuple-element.60) | copy-start | bytes 4116484
  59.0 4.3 %copy-start.4 = (f32[334,1024]{1,0:T(8,128)S(1)}, f32[334,1024]{1,0:T(8,128)}, u32[]{:S(2)}) copy-start(f32[334,1024]{1,0:T(8,128)} %get-tuple-element.55) | copy-start | bytes 4104196
  59.0 4.3 %copy-start.5 = (f32[334,1024]{1,0:T(8,128)S(1)}, f32[334,1024]{1,0:T(8,128)}, u32[]{:S(2)}) copy-start(f32[334,1024]{1,0:T(8,128)} %get-tuple-element.56) | copy-start | bytes 4104196
  59.0 4.3 %copy-start.6 = (f32[333,1024]{1,0:T(8,128)S(1)}, f32[333,1024]{1,0:T(8,128)}, u32[]{:S(2)}) copy-start(f32[333,1024]{1,0:T(8,128)} %get-tuple-element.51) | copy-start | bytes 4091908
  59.0 4.4 %copy-start.7 = (f32[333,1024]{1,0:T(8,128)S(1)}, f32[333,1024]{1,0:T(8,128)}, u32[]{:S(2)}) copy-start(f32[333,1024]{1,0:T(8,128)} %get-tuple-element.52) | copy-start | bytes 4091908
  59.0 4.8 %copy-start.8 = (f32[332,1024]{1,0:T(8,128)S(1)}, f32[332,1024]{1,0:T(8,128)}, u32[]{:S(2)}) copy-start(f32[332,1024]{1,0:T(8,128)} %get-tuple-element.47) | copy-start | bytes 4079620
  59.1 5.2 %copy-start.9 = (f32[332,1024]{1,0:T(8,128)S(1)}, f32[332,1024]{1,0:T(8,128)}, u32[]{:S(2)}) copy-start(f32[332,1024]{1,0:T(8,128)} %get-tuple-element.48) | copy-start | bytes 4079620
  69.2 1.1 copy-start.17
  69.2 2.4 copy-start.28
  73.7 1.0 copy-start.24
  75.0 1.9 copy-start.19
  77.2 1.1 copy-start.15
  77.7 1.2 copy-start.11
  80.4 1.0 copy-start.21
  80.4 1.5 copy-start.30
  (4 other events, 3.6 us)
Sparse Core Ops, SparseCore 0:
  10.1 48.8 all-gather.1

commit v2 on v1

--- a/solution.py
+++ b/solution.py
@@ -1,6 +1,10 @@
+import functools
+
 import jax
 import jax.numpy as jnp
 from jax import lax
+from jax.experimental import pallas as pl
+from jax.experimental.pallas import tpu as pltpu
 from jax.sharding import PartitionSpec as P
 
 EPSILON = 1e-05
@@ -56,6 +60,215 @@
         top = (2 * slot - 1) * bins
         total = total + wide[top : top + 3 * bins, slot * ch : (slot + 1) * ch]
     return total
+
+
+NX = 4
+CORES = 2
+PIECE = 96
+LANES = 256
+SUB = 8
+
+
+def row_loop(count, step, body):
+    lax.fori_loop(0, count // step, lambda i, carry: (body(pl.multiple_of(i * step, step)), carry)[1], 0)
+
+
+def sum_kernel(
+    nz, ny, one, two, three, lin, small, o_one, o_two, o_three, o_lin, o_small,
+    acc, out, snd, from_core, from_y, from_x, z_acc, z_snd, from_z, z_out, send_sem, recv_sem,
+):
+    dp, tm = lax.axis_index("dp"), lax.axis_index("tm")
+    z, x = dp // NX, dp % NX
+    y, core = tm // CORES, tm % CORES
+    chunk = NX * PIECE
+    half = ny * chunk
+
+    def at_core():
+        return (dp, y * CORES + (1 - core))
+
+    def at_y(d):
+        return (dp, ((y + d) % ny) * CORES + core)
+
+    def at_x(d):
+        return (z * NX + (x + d) % NX, tm)
+
+    def at_z(d):
+        return (((z + d) % nz) * NX + x, tm)
+
+    barrier = pltpu.get_barrier_semaphore()
+    peers = [at_z(d) for d in range(1, nz)] + [at_x(d) for d in range(1, NX)]
+    peers = peers + [at_y(d) for d in range(1, ny)] + [at_core()]
+    for peer in peers:
+        pl.semaphore_signal(barrier, inc=1, device_id=peer, device_id_type=pl.DeviceIdType.MESH)
+
+    first = 0
+    places = []
+    for src, dst in ((one, o_one), (two, o_two), (three, o_three), (lin, o_lin), (small, o_small)):
+        for lane in range(0, src.shape[1], LANES):
+            places.append((src, dst, lane, first, src.shape[0]))
+            first += src.shape[0]
+    for src, _, lane, top, count in places:
+        step = 16 if count % 48 else 48
+
+        def fill(i, src=src, lane=lane, top=top, step=step):
+            acc[pl.ds(top + i, step), :] = src[pl.ds(i, step), pl.ds(lane, LANES)]
+
+        row_loop(count, step, fill)
+    rest = acc.shape[0] - first
+    acc[pl.ds(first, rest), :] = jnp.zeros((rest, LANES), F32)
+
+    started = []
+
+    def send(src, dst, peer):
+        k = len(started)
+        copy = pltpu.make_async_remote_copy(
+            src_ref=src,
+            dst_ref=dst,
+            send_sem=send_sem.at[k],
+            recv_sem=recv_sem.at[k],
+            device_id=peer,
+            device_id_type=pl.DeviceIdType.MESH,
+        )
+        copy.start()
+        started.append(copy)
+        return copy
+
+    mine = core * half
+    theirs = (1 - core) * half
+    order = list(range(1, ny)) + [0]
+    pl.semaphore_wait(barrier, len(peers))
+    core_copies = []
+    for d in order:
+        place = pl.multiple_of(((y + d) % ny) * chunk, PIECE)
+
+        def narrow(i, place=place):
+            at = pl.multiple_of(theirs + place + i, 48)
+            snd[pl.ds(at, 48), :] = acc[pl.ds(at, 48), :].astype(BF)
+
+        row_loop(chunk, 48, narrow)
+        core_copies.append(
+            send(
+                snd.at[pl.ds(pl.multiple_of(theirs + place, PIECE), chunk)],
+                from_core.at[pl.ds(place, chunk)],
+                at_core(),
+            )
+        )
+    y_copies = []
+    for d, copy in zip(order, core_copies):
+        copy.wait_recv()
+        place = pl.multiple_of(((y + d) % ny) * chunk, PIECE)
+
+        def add_core(i, place=place, d=d):
+            at = pl.multiple_of(mine + place + i, 48)
+            total = acc[pl.ds(at, 48), :] + from_core[
+                pl.ds(pl.multiple_of(place + i, 48), 48), :
+            ].astype(F32)
+            if d == 0:
+                acc[pl.ds(at, 48), :] = total
+            else:
+                snd[pl.ds(at, 48), :] = total.astype(BF)
+
+        row_loop(chunk, 48, add_core)
+        if d:
+            y_copies.append(
+                send(
+                    snd.at[pl.ds(pl.multiple_of(mine + place, PIECE), chunk)],
+                    from_y.at[d - 1],
+                    at_y(d),
+                )
+            )
+    for copy in y_copies:
+        copy.wait_recv()
+    own = pl.multiple_of(mine + y * chunk, PIECE)
+
+    def add_y(i):
+        at = pl.multiple_of(own + i, 48)
+        total = acc[pl.ds(at, 48), :]
+        for d in range(1, ny):
+            total = total + from_y[d - 1, pl.ds(i, 48), :].astype(F32)
+        acc[pl.ds(at, 48), :] = total
+        snd[pl.ds(at, 48), :] = total.astype(BF)
+
+    row_loop(chunk, 48, add_y)
+    x_copies = []
+    for d in range(1, NX):
+        place = pl.multiple_of(own + ((x + d) % NX) * PIECE, PIECE)
+        x_copies.append(send(snd.at[pl.ds(place, PIECE)], from_x.at[d - 1], at_x(d)))
+    for copy in x_copies:
+        copy.wait_recv()
+    piece = pl.multiple_of(own + x * PIECE, PIECE)
+    total = acc[pl.ds(piece, PIECE), :]
+    for d in range(1, NX):
+        total = total + from_x[d - 1].astype(F32)
+    parts = PIECE // SUB
+    total = total.reshape(parts, SUB, LANES)
+    z_acc[pl.ds(0, parts)] = total
+    z_snd[pl.ds(0, parts)] = total.astype(BF)
+    z_acc[pl.ds(parts, nz - parts)] = jnp.zeros((nz - parts, SUB, LANES), F32)
+    z_snd[pl.ds(parts, nz - parts)] = jnp.zeros((nz - parts, SUB, LANES), BF)
+    far = sorted(range(1, nz), key=lambda d: -min(d, nz - d))
+    z_copies = [send(z_snd.at[(z + d) % nz], from_z.at[d - 1], at_z(d)) for d in far]
+    for copy in z_copies:
+        copy.wait_recv()
+    total = z_acc[z]
+    for d in range(1, nz):
+        total = total + from_z[d - 1].astype(F32)
+    z_out[z] = total.astype(BF)
+    z_copies = [send(z_out.at[z], z_out.at[z], at_z(d)) for d in far]
+    for copy in z_copies:
+        copy.wait_recv()
+    done = z_out[pl.ds(0, parts)].astype(F32).reshape(PIECE, LANES)
+    out[pl.ds(piece, PIECE), :] = done.astype(BF)
+    whole = out.at[pl.ds(piece, PIECE)]
+    x_copies = [send(whole, whole, at_x(d)) for d in range(1, NX)]
+    for copy in x_copies:
+        copy.wait_recv()
+    whole = out.at[pl.ds(own, chunk)]
+    y_copies = [send(whole, whole, at_y(d)) for d in range(1, ny)]
+    core_copies = [send(whole, whole, at_core())]
+    for d, copy in zip(range(1, ny), y_copies):
+        copy.wait_recv()
+        place = pl.multiple_of(mine + ((y - d + ny) % ny) * chunk, PIECE)
+        whole = out.at[pl.ds(place, chunk)]
+        core_copies.append(send(whole, whole, at_core()))
+    for copy in core_copies:
+        copy.wait_recv()
+    for copy in started:
+        copy.wait_send()
+    for _, dst, lane, top, count in places:
+        step = 16 if count % 48 else 48
+
+        def drain(i, dst=dst, lane=lane, top=top, step=step):
+            dst[pl.ds(i, step), pl.ds(lane, LANES)] = out[pl.ds(top + i, step), :]
+
+        row_loop(count, step, drain)
+
+
+def sum_everywhere(pieces, nz, ny):
+    total = CORES * ny * NX * PIECE
+    copies = 2 * (ny + (ny - 1) + (NX - 1) + (nz - 1))
+    vmem = pl.BlockSpec(memory_space=pltpu.VMEM)
+    return pl.pallas_call(
+        functools.partial(sum_kernel, nz, ny),
+        out_shape=[jax.ShapeDtypeStruct(p.shape, BF) for p in pieces],
+        in_specs=[vmem] * len(pieces),
+        out_specs=[vmem] * len(pieces),
+        scratch_shapes=[
+            pltpu.VMEM((total, LANES), F32),
+            pltpu.VMEM((total, LANES), BF),
+            pltpu.VMEM((total, LANES), BF),
+            pltpu.VMEM((total // CORES, LANES), BF),
+            pltpu.VMEM((ny - 1, NX * PIECE, LANES), BF),
+            pltpu.VMEM((NX - 1, PIECE, LANES), BF),
+            pltpu.VMEM((nz, SUB, LANES), F32),
+            pltpu.VMEM((nz, SUB, LANES), BF),
+            pltpu.VMEM((nz - 1, SUB, LANES), BF),
+            pltpu.VMEM((nz, SUB, LANES), BF),
+            pltpu.SemaphoreType.DMA((copies,)),
+            pltpu.SemaphoreType.DMA((copies,)),
+        ],
+        compiler_params=pltpu.CompilerParams(collective_id=0, has_side_effects=True),
+    )(*pieces)
 
 
 def per_device(
@@ -171,10 +384,13 @@
     )
     ez1 = through_silu(da1, z1)
     grad_one = narrow_conv_one(mm_tn(x_wide, ez1))
-    summed = lax.psum(
-        (grad_one, grad_two, grad_three, grad_lin, grad_gain, grad_bias, grad_kernel), ("dp", "tm")
-    )
-    return tuple(piece.astype(BF) for piece in summed)
+    small = jnp.concatenate(
+        [grad_kernel, grad_gain[None], grad_bias[None], jnp.zeros((16 - taps - 2, width), F32)], axis=0
+    )
+    one, two, three, lin, small = sum_everywhere(
+        (grad_one, grad_two, grad_three, grad_lin, small), dp_count // NX, tm_count // CORES
+    )
+    return (one, two, three, lin, small[taps], small[taps + 1], small[:taps])
 
 
 def solution(mesh):

time: 279 us -> 172 us (0.62)
  blocking collectives: 182 us -> 0 us
  Pallas kernels: 0 us -> 62.4 us
  local copies, waits for them, and re-layouts: 18.1 us -> 28.1 us
    psum x1 -> x0, blocking collectives: 182 us -> none  [per_device(): lax.psum((grad_one, grad_two, grad_three, grad_lin, grad_gain, grad_bias,...]
    pallas_call x0 -> x1, Pallas kernels: none -> 62.4 us  [sum_everywhere(): pl.pallas_call(functools.partial(sum_kernel, nz, ny), out_shape=[jax.Shap...]
    unnamed x62 -> x71, local copies, waits for them, and re-layouts: 6.41 us -> 13.8 us
  transfers between devices with their start and end apart: 3 -> 3, of which waited for: 1 -> 1; matrix products, arithmetic and copies ran while one was open for 6% -> 10% of each run, Pallas kernels for 0% -> 0%
where the time goes in v2:
time: 172 us; the launch traced here: 171 us
  Pallas kernels  62.4 us (36%)
  local copies, waits for them, and re-layouts  28.1 us (16%)
  waiting for transfers between devices  22.7 us (13%)
  matrix products  16.7 us (10%)
  between operations  15.5 us (9%)
  other arithmetic  15.2 us (9%)
  starting transfers between devices  10.7 us (6%)
    pallas_call x1, Pallas kernels, sum_everywhere(): pl.pallas_call(functools.partial(sum_kernel, nz, ny), out_shape=[jax.Shap...  62.4 us
    all_gather x1, waiting for transfers between devices, per_device(): proj_full = lax.all_gather(proj, 'tm', axis=1, tiled=True)  22 us
    unnamed x71, local copies, waits for them, and re-layouts  13.8 us
    ppermute x1, starting transfers between devices, per_device(): after = lax.ppermute(mel[0, :half], 'tm', down)  8.73 us
    slice x26, local copies, waits for them, and re-layouts, roll(): return jnp.roll(values, shift, axis=0)  8.46 us
    dot_general x8, matrix products, mm(): return jnp.dot(lhs, rhs, preferred_element_type=F32)  7.77 us
    dot_general x7, matrix products, mm_tn(): lax.dot_general(lhs, rhs, (((0,), (0,)), ((), ())), preferred_element_typ...  5.14 us
    another operation x1, other arithmetic  4.95 us
  transfers between devices with their start and end apart: 3, of which 1 were waited for; matrix products, arithmetic and copies ran while one was open for 10% of the time, Pallas kernels for 0%

profile of v2, /device:TPU:1, one launch (start us, length us, event | category | flops | bytes accessed | tf_op | source)
XLA Modules:
  0.0 171.4 jit_solution(691489807861469676)
XLA Ops:
  7.9 0.7 slice_bitcast_fusion
  8.6 8.7 %collective-permute-start = (bf16[4,640]{1,0:T(4,128)(2,1)S(1)}, bf16[4,640]{1,0:T(4,128)(2,1)S(1)}, u32[]{:S(2)}, u32[]{:S(2)}) collective-permute-start(bf16[4,640]{1,0:T(4,128)(2,1)S(1)} %slice_bitcast_fusion), channel_id=1, source_target_pairs={{1,0},{2,1},{3,2},{4,3},{5,4},{6,5},{7,6},{9,8},{10,9},{11,10},{12... | collective-permute-start | bytes 15368 | tf_op jit(solution)/shard_map/ppermute | solution.py:307
  17.4 1.2 dynamic_slice.8
  19.3 0.7 dynamic-slice_bitcast_fusion
  20.0 1.9 %collective-permute-start.1 = (bf16[5,640]{1,0:T(8,128)(2,1)S(1)}, bf16[5,640]{1,0:T(8,128)(2,1)S(1)}, u32[]{:S(2)}, u32[]{:S(2)}) collective-permute-start(bf16[5,640]{1,0:T(8,128)(2,1)S(1)} %dynamic-slice_bitcast_fusion), channel_id=1, source_target_pairs={{0,1},{1,2},{2,3},{3,4},{4,5},{5,6},{6,7},{8,9},{9,10},{10,11},{11... | collective-permute-start | bytes 19208 | tf_op jit(solution)/shard_map/ppermute | solution.py:306
  22.0 0.8 convert_element_type.65
  22.8 1.3 convert_multiply_fusion.1
  24.3 1.4 fusion.147
  25.7 1.8 %fusion.149 = (f32[333,1024]{1,0:T(8,128)}, f32[333,1024]{1,0:T(8,128)}) fusion(f32[336,1024]{1,0:T(8,128)S(1)} %convert_multiply_fusion.1), kind=kLoop, calls=%fused_computation.204 | loop fusion | bytes 5455872 | tf_op jit(solution)/shard_map/jit(_roll_static)/slice | solution.py:28
  27.5 1.8 %fusion.151 = (f32[334,1024]{1,0:T(8,128)}, f32[334,1024]{1,0:T(8,128)}) fusion(f32[336,1024]{1,0:T(8,128)S(1)} %convert_multiply_fusion.1), kind=kLoop, calls=%fused_computation.206 | loop fusion | bytes 5472256 | tf_op jit(solution)/shard_map/jit(_roll_static)/slice | solution.py:28
  29.2 1.8 %fusion.153 = (f32[335,1024]{1,0:T(8,128)}, f32[335,1024]{1,0:T(8,128)}) fusion(f32[336,1024]{1,0:T(8,128)S(1)} %convert_multiply_fusion.1), kind=kLoop, calls=%fused_computation.208 | loop fusion | bytes 5488640 | tf_op jit(solution)/shard_map/jit(_roll_static)/slice | solution.py:28
  31.7 1.9 %multiply_convert_fusion.2 = (bf16[336,1024]{1,0:T(8,128)(2,1)S(1)}, f32[336,1024]{1,0:T(8,128)}) fusion(bf16[240,256]{1,0:T(8,128)(2,1)S(1)} %copy-done.27, bf16[80,256]{1,0:T(8,128)(2,1)S(1)} %slice-done.1, bf16[480,256]{1,0:T(8,128)(2,1)S(1)} %broadcast_in_dim.62, bf16[160,256]{1,0:T(8,128)(2,1)S(1)} %slice-done, bf16[335,80]{1,0:T(8,128)(2,1)S(1)} %slice.365, ...), kind=kOutput, calls=%fused_computation.94 | convolution fusion | flops 514844160 | bytes 3039744 | tf_op jit(solution)/shard_map/dot_general | solution.py:16
  37.1 22.0 %all-gather.2.cloned.1.call-done = bf16[1024,2048]{1,0:T(8,128)(2,1)} async-done(((bf16[1024,256]{1,0:T(8,128)(2,1)}), bf16[1024,2048]{1,0:T(8,128)(2,1)}) %all-gather.2.cloned.1.call-update) | async-done | bytes 4194320 | tf_op jit(solution)/shard_map/all_gather | solution.py:302
  59.1 4.2 %fusion.76 = f32[336,2048]{1,0:T(8,128)S(1)} fusion(bf16[1024,2048]{1,0:T(8,128)(2,1)} %all-gather.2.cloned.1.call-done, bf16[336,1024]{1,0:T(8,128)(2,1)} %copy-done.16, f32[1024]{0:T(1024)S(1)} %copy-done.31, f32[1024]{0:T(1024)S(1)} %copy-done.29, f32[336]{0:T(512)S(1)} %add_rsqrt_fusion, f32[336]{0:T(512)S(1)} %broadcast_multiply_fusion.2), kind=kOutput, calls=%fused_computation.107 | convolution fusion | flops 1411350528 | bytes 7645824 | tf_op jit(solution)/shard_map/dot_general | solution.py:16
  64.3 5.0 %fusion.73 = (bf16[336,1024]{1,0:T(8,128)(2,1)S(1)}, bf16[336,1024]{1,0:T(8,128)(2,1)S(1)}) fusion(f32[336,2048]{1,0:T(8,128)S(1)} %fusion.76, f32[1024]{0:T(1024)S(1)} %bitcast.53, f32[332,1024]{1,0:T(8,128)S(1)} %copy-done.3, f32[4,1024]{1,0:T(4,128)S(1)} %get-tuple-element.55, f32[1024]{0:T(1024)S(1)} %bitcast.52, f32[333,1024]{1,0:T(8,128)S(1)} %copy-done.5, ...), kind=kLoop, calls=%fused_computation.93 | loop fusion | flops 12042240 | bytes 14455456 | tf_op jit(solution)/shard_map/convert
  72.1 1.3 copy-done.30
  73.4 2.0 %fusion.44 = (f32[1024]{0:T(1024)S(1)}, f32[336]{0:T(512)S(1)}, f32[336]{0:T(512)S(1)}, f32[1024]{0:T(1024)S(1)}, f32[336,1024]{1,0:T(8,128)S(1)}) fusion(bf16[336,1024]{1,0:T(8,128)(2,1)S(1)} %copy-done.17, f32[336]{0:T(512)S(1)} %add_rsqrt_fusion, f32[336]{0:T(512)S(1)} %broadcast_multiply_fusion.2, f32[1024]{0:T(1024)S(1)} %copy-done.29, ...), kind=kOutput, calls=%fused_computation.50 | convolution fusion | flops 1415476480 | bytes 7652608 | tf_op jit(solution)/shard_map/dot_general | solution.py:24
  81.4 0.9 copy-done.21
  82.8 1.1 fusion.83
  84.0 1.5 fusion.137.lin
  85.4 0.9 pad_maximum_fusion.three
  86.4 1.3 convolution_add_fusion.two
  87.7 0.8 slice_add_fusion.1.one
  88.5 1.0 fusion.48
  89.5 3.4 %fusion.54 = (f32[1024]{0:T(1024)S(1)}, f32[1024]{0:T(1024)S(1)}, f32[1024]{0:T(1024)S(1)}, f32[1024]{0:T(1024)S(1)}, f32[1024]{0:T(1024)S(1)}, /*index=5*/f32[1024]{0:T(1024)S(1)}) fusion(f32[4,1024]{1,0:T(4,128)S(1)} %get-tuple-element.50, f32[332,1024]{1,0:T(8,128)S(1)} %get-tuple-element.48, bf16[320,1024]{1,0:T(8,128)(2,1)S(1)} %bitcast.43, ...), kind=kLoop, calls=%fused_computation.60 | loop fusion | flops 6875136 | bytes 8937808 | tf_op jit(solution)/shard_map/reduce_sum | solution.py:349
  92.9 1.3 concatenate.139.small
  94.2 62.4 %shard_map.162 = (bf16[240,256]{1,0:T(8,128)(2,1)}, bf16[768,256]{1,0:T(8,128)(2,1)}, bf16[768,256]{1,0:T(8,128)(2,1)}, bf16[256,1024]{1,0:T(8,128)(2,1)}, bf16[16,1024]{1,0:T(8,128)(2,1)}) custom-call(f32[240,256]{1,0:T(8,128)} %slice_add_fusion.1.one, f32[768,256]{1,0:T(8,128)} %convolution_add_fusion.two, f32[768,256]{1,0:T(8,128)} %pad_maximum_fusion.three, ...), custom_call_target="tpu_custom_call" | custom-call | tf_op jit(solution)/shard_map/pallas_call | solution.py:251
  156.6 1.4 slice_reduce_fusion
  158.0 1.6 copy.25
  159.6 1.8 %copy.26 = bf16[768,256]{1,0:T(8,128)(2,1)} copy(bf16[768,256]{1,0:T(8,128)(2,1)} %get-tuple-element.94) | data formatting | bytes 786432
  161.3 1.8 %copy.27 = bf16[768,256]{1,0:T(8,128)(2,1)} copy(bf16[768,256]{1,0:T(8,128)(2,1)} %get-tuple-element.95) | data formatting | bytes 786432
  163.1 0.8 copy.28
  (132 shorter events, 15.4 us)
Async XLA Ops:
  7.2 28.5 %copy-start = (bf16[256,1024]{1,0:T(8,128)(2,1)S(1)}, bf16[256,1024]{1,0:T(8,128)(2,1)}, u32[]{:S(2)}) copy-start(bf16[256,1024]{1,0:T(8,128)(2,1)} %param.16) | copy-start | bytes 1572868
  7.2 17.0 %copy-start.23 = (bf16[1,320,640]{2,1,0:T(8,128)(2,1)S(1)}, bf16[1,320,640]{2,1,0:T(8,128)(2,1)}, u32[]{:S(2)}) copy-start(bf16[1,320,640]{2,1,0:T(8,128)(2,1)} %param.11) | copy-start | bytes 1228804
  7.2 16.9 %copy-start.26 = (bf16[9,1024]{1,0:T(8,128)(2,1)S(1)}, bf16[9,1024]{1,0:T(8,128)(2,1)}, u32[]{:S(2)}) copy-start(bf16[9,1024]{1,0:T(8,128)(2,1)} %param.20) | copy-start | bytes 55300
  7.2 51.9 %all-gather.2.cloned.1.call-start = ((), (), s32[]{:S(2)}) async-start(), calls=%async_computation | async-start | bytes 4718592 | tf_op jit(solution)/shard_map/all_gather | solution.py:302
  8.6 22.4 %collective-permute-start = (bf16[4,640]{1,0:T(4,128)(2,1)S(1)}, bf16[4,640]{1,0:T(4,128)(2,1)S(1)}, u32[]{:S(2)}, u32[]{:S(2)}) collective-permute-start(bf16[4,640]{1,0:T(4,128)(2,1)S(1)} %slice_bitcast_fusion), channel_id=1, source_target_pairs={{1,0},{2,1},{3,2},{4,3},{5,4},{6,5},{7,6},{9,8},{10,9},{11,10},{12... | collective-permute-start | bytes 15368 | tf_op jit(solution)/shard_map/ppermute | solution.py:307
  20.0 11.2 %collective-permute-start.1 = (bf16[5,640]{1,0:T(8,128)(2,1)S(1)}, bf16[5,640]{1,0:T(8,128)(2,1)S(1)}, u32[]{:S(2)}, u32[]{:S(2)}) collective-permute-start(bf16[5,640]{1,0:T(8,128)(2,1)S(1)} %dynamic-slice_bitcast_fusion), channel_id=1, source_target_pairs={{0,1},{1,2},{2,3},{3,4},{4,5},{5,6},{6,7},{8,9},{9,10},{10,11},{11... | collective-permute-start | bytes 19208 | tf_op jit(solution)/shard_map/ppermute | solution.py:306
  29.2 2.4 %copy-start.27 = (bf16[240,256]{1,0:T(8,128)(2,1)S(1)}, bf16[240,256]{1,0:T(8,128)(2,1)}, u32[]{:S(2)}) copy-start(bf16[240,256]{1,0:T(8,128)(2,1)} %param.13) | copy-start | bytes 368644
  29.2 2.4 %slice-start = ((bf16[240,256]{1,0:T(8,128)(2,1)}), bf16[160,256]{1,0:T(8,128)(2,1)S(1)}, s32[]{:S(2)}) async-start(bf16[240,256]{1,0:T(8,128)(2,1)} %param.13), calls=%async_computation.1 | async-start | bytes 163840 | tf_op jit(solution)/shard_map/slice | solution.py:46
  29.2 2.4 %slice-start.1 = ((bf16[240,256]{1,0:T(8,128)(2,1)}), bf16[80,256]{1,0:T(8,128)(2,1)S(1)}, s32[]{:S(2)}) async-start(bf16[240,256]{1,0:T(8,128)(2,1)} %param.13), calls=%async_computation.2 | async-start | bytes 81920 | tf_op jit(solution)/shard_map/slice | solution.py:46
  31.4 2.1 %copy-start.20 = (bf16[336,640]{1,0:T(8,128)(2,1)}, bf16[336,640]{1,0:T(8,128)(2,1)S(1)}, u32[]{:S(2)}) copy-start(bf16[336,640]{1,0:T(8,128)(2,1)S(1)} %dynamic_update_slice.7) | copy-start | bytes 1290244
  31.7 1.9 %copy-start.2 = (bf16[768,256]{1,0:T(8,128)(2,1)S(1)}, bf16[768,256]{1,0:T(8,128)(2,1)}, u32[]{:S(2)}) copy-start(bf16[768,256]{1,0:T(8,128)(2,1)} %param.14) | copy-start | bytes 1179652
  34.1 1.4 copy-start.12
  34.1 1.1 copy-start.18
  34.4 1.3 copy-start.14
  35.7 23.4 %copy-start.29 = (f32[1024]{0:T(1024)S(1)}, f32[1024]{0:T(1024)}, u32[]{:S(2)}) copy-start(f32[1024]{0:T(1024)} %param.17) | copy-start | bytes 12292
  35.7 23.4 %copy-start.31 = (f32[1024]{0:T(1024)S(1)}, f32[1024]{0:T(1024)}, u32[]{:S(2)}) copy-start(f32[1024]{0:T(1024)} %param.18) | copy-start | bytes 12292
  37.1 26.3 %copy-start.1 = (bf16[1,320,1024]{2,1,0:T(8,128)(2,1)S(1)}, bf16[1,320,1024]{2,1,0:T(8,128)(2,1)}, u32[]{:S(2)}) copy-start(bf16[1,320,1024]{2,1,0:T(8,128)(2,1)} %param.12) | copy-start | bytes 1966084
  59.1 4.3 %copy-start.3 = (f32[332,1024]{1,0:T(8,128)S(1)}, f32[332,1024]{1,0:T(8,128)}, u32[]{:S(2)}) copy-start(f32[332,1024]{1,0:T(8,128)} %get-tuple-element.53) | copy-start | bytes 4079620
  59.1 4.3 %copy-start.4 = (f32[333,1024]{1,0:T(8,128)S(1)}, f32[333,1024]{1,0:T(8,128)}, u32[]{:S(2)}) copy-start(f32[333,1024]{1,0:T(8,128)} %get-tuple-element.56) | copy-start | bytes 4091908
  59.1 4.3 %copy-start.5 = (f32[333,1024]{1,0:T(8,128)S(1)}, f32[333,1024]{1,0:T(8,128)}, u32[]{:S(2)}) copy-start(f32[333,1024]{1,0:T(8,128)} %get-tuple-element.57) | copy-start | bytes 4091908
  59.1 4.3 %copy-start.6 = (f32[334,1024]{1,0:T(8,128)S(1)}, f32[334,1024]{1,0:T(8,128)}, u32[]{:S(2)}) copy-start(f32[334,1024]{1,0:T(8,128)} %get-tuple-element.60) | copy-start | bytes 4104196
  59.1 4.4 %copy-start.7 = (f32[334,1024]{1,0:T(8,128)S(1)}, f32[334,1024]{1,0:T(8,128)}, u32[]{:S(2)}) copy-start(f32[334,1024]{1,0:T(8,128)} %get-tuple-element.61) | copy-start | bytes 4104196
  59.1 4.8 %copy-start.8 = (f32[335,1024]{1,0:T(8,128)S(1)}, f32[335,1024]{1,0:T(8,128)}, u32[]{:S(2)}) copy-start(f32[335,1024]{1,0:T(8,128)} %get-tuple-element.64) | copy-start | bytes 4116484
  59.1 5.2 %copy-start.9 = (f32[335,1024]{1,0:T(8,128)S(1)}, f32[335,1024]{1,0:T(8,128)}, u32[]{:S(2)}) copy-start(f32[335,1024]{1,0:T(8,128)} %get-tuple-element.65) | copy-start | bytes 4116484
  71.0 1.1 copy-start.17
  71.0 2.4 %copy-start.30 = (bf16[1024,2048]{1,0:T(8,128)(2,1)S(1)}, bf16[1024,2048]{1,0:T(8,128)(2,1)}, u32[]{:S(2)}) copy-start(bf16[1024,2048]{1,0:T(8,128)(2,1)} %all-gather.2.cloned.1.call-done) | copy-start | bytes 12582916
  78.1 1.1 copy-start.15
  78.7 1.2 copy-start.11
  81.3 1.0 copy-start.21
  81.3 1.5 copy-start.32
  156.6 6.5 %copy-start.22 = (bf16[256,1024]{1,0:T(8,128)(2,1)S(1)}, bf16[256,1024]{1,0:T(8,128)(2,1)}, u32[]{:S(2)}) copy-start(bf16[256,1024]{1,0:T(8,128)(2,1)} %get-tuple-element.96) | copy-start | bytes 1572868
  158.0 5.9 %copy-start.28 = (bf16[16,1024]{1,0:T(8,128)(2,1)S(1)}, bf16[16,1024]{1,0:T(8,128)(2,1)}, u32[]{:S(2)}) copy-start(bf16[16,1024]{1,0:T(8,128)(2,1)} %get-tuple-element.16) | copy-start | bytes 98308
  (6 other events, 5.5 us)
Sparse Core Ops, SparseCore 0:
  10.1 48.9 all-gather.1

commit v3 on v2

--- a/solution.py
+++ b/solution.py
@@ -24,10 +24,6 @@
     return lax.dot_general(lhs, rhs, (((1,), (1,)), ((), ())), preferred_element_type=F32)
 
 
-def roll(values, shift):
-    return jnp.roll(values, shift, axis=0)
-
-
 def silu(z):
     return (z * jax.nn.sigmoid(z)).astype(BF)
 
@@ -38,28 +34,17 @@
 
 
 def wide_conv_one(conv):
-    bins = conv.shape[0] // 3
-    columns = []
-    for slot in range(4):
-        if slot == 0:
-            column = jnp.concatenate(
-                [conv[bins:], jnp.zeros((6 * bins, conv.shape[1]), conv.dtype), conv[:bins]], axis=0
-            )
-        else:
-            top = (2 * slot - 1) * bins
-            column = jnp.pad(conv, ((top, 9 * bins - top - 3 * bins), (0, 0)))
-        columns.append(column)
-    return jnp.concatenate(columns, axis=1)
-
-
-def narrow_conv_one(wide):
-    bins = wide.shape[0] // 9
-    ch = wide.shape[1] // 4
-    total = jnp.concatenate([wide[8 * bins :, :ch], wide[: 2 * bins, :ch]], axis=0)
+    bins, ch = conv.shape[0] // 3, conv.shape[1]
+    rows = 768
+
+    def zeros(count):
+        return jnp.zeros((count, ch), conv.dtype)
+
+    columns = [jnp.concatenate([conv[bins:], zeros(rows - 3 * bins), conv[:bins]], axis=0)]
     for slot in range(1, 4):
         top = (2 * slot - 1) * bins
-        total = total + wide[top : top + 3 * bins, slot * ch : (slot + 1) * ch]
-    return total
+        columns.append(jnp.pad(conv, ((top, rows - top - 3 * bins), (0, 0))))
+    return jnp.concatenate(columns, axis=1)
 
 
 NX = 4
@@ -271,6 +256,295 @@
     )(*pieces)
 
 
+ROWS = 336
+STEP = 48
+RIM = 16
+
+
+def work_kernel(
+    tm_n, half, scale, live_ref, mel, cot, proj, w_one, w_two, w_three, lin, gain, bias, taps,
+    one, two, three, g_lin, small,
+    full, xw, up_snd, up_rcv, down_rcv, z1, z2, z3, a1, a2, a3, n_ref, inv_ref, u_ref, du_ref,
+    eg_ref, gated_ref, em, dh_ref, sums, own_sem, send_sem, recv_sem,
+):
+    dp, tm = lax.axis_index("dp"), lax.axis_index("tm")
+    ny = tm_n // CORES
+    y, core = tm // CORES, tm % CORES
+    own_rows = mel.shape[0]
+    width = lin.shape[1]
+    live = live_ref[0]
+
+    def at(d):
+        return (dp, (tm + d) % tm_n)
+
+    barrier = pltpu.get_barrier_semaphore()
+    for d in range(1, tm_n):
+        pl.semaphore_signal(barrier, inc=1, device_id=at(d), device_id_type=pl.DeviceIdType.MESH)
+
+    first_row = lax.broadcasted_iota(jnp.int32, (RIM, own_rows), 0)
+    column = lax.broadcasted_iota(jnp.int32, (RIM, own_rows), 1)
+    pick = (column - live == first_row - RIM) & (first_row >= RIM - half - 1)
+    up_snd[...] = mm(pick.astype(F32).astype(BF), mel[...]).astype(BF)
+    pl.semaphore_wait(barrier, tm_n - 1)
+
+    started = []
+
+    def send(src, dst, peer):
+        k = len(started)
+        copy = pltpu.make_async_remote_copy(
+            src_ref=src,
+            dst_ref=dst,
+            send_sem=send_sem.at[k],
+            recv_sem=recv_sem.at[k],
+            device_id=peer,
+            device_id_type=pl.DeviceIdType.MESH,
+        )
+        copy.start()
+        started.append(copy)
+        return copy
+
+    partner = (dp, y * CORES + (1 - core))
+    up = send(up_snd, up_rcv, at(1))
+    down = send(mel.at[pl.ds(0, RIM)], down_rcv, at(tm_n - 1))
+    y_copies = [(d, send(proj, full.at[tm], (dp, ((y + d) % ny) * CORES + core))) for d in (1, 3, 2)]
+    core_copies = [send(proj, full.at[tm], partner)]
+    keep = pltpu.make_async_copy(proj, full.at[tm], own_sem)
+    keep.start()
+
+    def mask(count, lanes):
+        ids = lax.broadcasted_iota(jnp.int32, (count, lanes), 0)
+        right = (ids < live + half) & (tm < tm_n - 1)
+        left = (ids >= ROWS - half) & (tm > 0)
+        return (ids < live) | right | left
+
+    def cot_block(cols):
+        c = cot[:, cols].astype(F32) * scale
+        ids = lax.broadcasted_iota(jnp.int32, c.shape, 0)
+        c = jnp.where(ids < live, c, 0.0)
+        return jnp.concatenate([c, jnp.zeros((ROWS - own_rows, c.shape[1]), F32)], axis=0)
+
+    def back_taps(i, carry):
+        cols = pl.ds(pl.multiple_of(i * 128, 128), 128)
+        c = cot_block(cols)
+        total = jnp.zeros_like(c)
+        for k in range(2 * half + 1):
+            shifted = pltpu.roll(c, (k - half) % ROWS, 0) if k != half else c
+            total = total + shifted * taps[k : k + 1, cols]
+        eg_ref[:, cols] = jnp.where(mask(ROWS, 128), total, 0.0).astype(BF)
+        return carry
+
+    lax.fori_loop(0, width // 128, back_taps, 0)
+
+    up.wait_recv()
+    down.wait_recv()
+
+    def place(i, carry):
+        at_row = pl.multiple_of(i * 64, 64)
+        rows = lax.broadcasted_iota(jnp.int32, (64, RIM), 0) + at_row
+        slot = lax.broadcasted_iota(jnp.int32, (64, RIM), 1)
+        pick = (rows - live == slot) & (slot < half) & (tm < tm_n - 1)
+        ids = lax.broadcasted_iota(jnp.int32, (64, mel.shape[1]), 0) + at_row
+        value = jnp.where(ids < live, mel[pl.ds(at_row, 64), :].astype(F32), 0.0)
+        value = value + mm(pick.astype(F32).astype(BF), down_rcv[...])
+        xw[pl.ds(at_row, 64), 0:640] = value.astype(BF)
+        return carry
+
+    lax.fori_loop(0, own_rows // 64, place, 0)
+    rows = lax.broadcasted_iota(jnp.int32, (RIM, RIM), 0) + own_rows
+    slot = lax.broadcasted_iota(jnp.int32, (RIM, RIM), 1)
+    pick = (rows - live == slot) & (slot < half) & (tm < tm_n - 1)
+    value = mm(pick.astype(F32).astype(BF), down_rcv[...])
+    value = value + jnp.where(tm > 0, 1.0, 0.0) * up_rcv[...].astype(F32)
+    xw[own_rows:ROWS, 0:640] = value.astype(BF)
+    xw[:, 640:768] = pltpu.roll(xw[:, 512:640].astype(F32), 1, 0).astype(BF)
+
+    windows = ((0, 256), (0, 384), (128, 512), (384, 640))
+    for j, (low, high) in enumerate(windows):
+        cols = slice(256 * j, 256 * j + 256)
+        z = mm(xw[:, low:high], w_one[low:high, cols])
+        if j == 0:
+            z = z + mm(xw[:, 640:768], w_one[640:768, cols])
+        z1[:, cols] = z
+        a1[:, cols] = silu(z)
+    z = mm(a1[:, :512], w_two[256:, :]) + pltpu.roll(mm(a1[:, 768:], w_two[:256, :]), 1, 0)
+    z2[:, :256] = z
+    a2[:, :256] = silu(z)
+    z = mm(a1[:, 256:], w_two[...])
+    z2[:, 256:] = z
+    a2[:, 256:] = silu(z)
+    z = mm(a2[...], w_three[256:, :]) + pltpu.roll(mm(a2[:, 256:], w_three[:256, :]), 1, 0)
+    z3[...] = z
+    a3[...] = silu(z)
+
+    def project(i, carry):
+        cols = pl.ds(pl.multiple_of(i * 256, 256), 256)
+        n_ref[:, cols] = mm(a3[...], lin[:, cols]).astype(BF).astype(F32)
+        return carry
+
+    lax.fori_loop(0, width // 256, project, 0)
+
+    def normalise(i, carry):
+        rows = pl.ds(pl.multiple_of(i * STEP, STEP), STEP)
+        h = n_ref[rows, :]
+        h = h - jnp.mean(h, axis=-1, keepdims=True)
+        inverse = lax.rsqrt(jnp.mean(h * h, axis=-1, keepdims=True) + EPSILON)
+        n = h * inverse
+        n_ref[rows, :] = n
+        inv_ref[rows, :] = jnp.broadcast_to(inverse, (STEP, 128))
+        u_ref[rows, :] = (n * gain[...] + bias[...]).astype(BF)
+        return carry
+
+    lax.fori_loop(0, ROWS // STEP, normalise, 0)
+
+    for d, copy in y_copies:
+        copy.wait_recv()
+        came = ((y - d + ny) % ny) * CORES + core
+        core_copies.append(send(full.at[came], full.at[came], partner))
+    keep.wait()
+    for copy in core_copies:
+        copy.wait_recv()
+
+    def gates(i, carry):
+        cols = pl.ds(pl.multiple_of(i * 256, 256), 256)
+        value = mm(u_ref[...], full[i])
+        gate = jax.nn.sigmoid(mm(u_ref[...], full[i + ny]))
+        gated = (value * gate).astype(BF).astype(F32)
+        gated_ref[:, cols] = jnp.where(mask(ROWS, 256), gated, 0.0)
+        grad = eg_ref[:, cols].astype(F32) * gate
+        em[i] = grad.astype(BF)
+        em[i + ny] = (grad * value * (1.0 - gate)).astype(BF)
+        return carry
+
+    lax.fori_loop(0, width // 256, gates, 0)
+
+    def tap_grads(i, carry):
+        cols = pl.ds(pl.multiple_of(i * 128, 128), 128)
+        c = cot_block(cols)
+        gated = gated_ref[:, cols]
+        sums_k = []
+        for k in range(2 * half + 1):
+            shifted = pltpu.roll(c, (k - half) % ROWS, 0) if k != half else c
+            sums_k.append(jnp.sum(gated * shifted, axis=0, keepdims=True))
+        sums_k.append(jnp.zeros((16 - len(sums_k), 128), F32))
+        small[:, cols] = jnp.concatenate(sums_k, axis=0)
+        return carry
+
+    lax.fori_loop(0, width // 128, tap_grads, 0)
+
+    def unproject(i, carry):
+        cols = pl.multiple_of(i * 256, 256)
+        total = mm_nt(em[0], full[0, pl.ds(cols, 256), :])
+        for t in range(1, tm_n):
+            total = total + mm_nt(em[t], full[t, pl.ds(cols, 256), :])
+        du_ref[:, pl.ds(cols, 256)] = total
+        return carry
+
+    lax.fori_loop(0, width // 256, unproject, 0)
+    sums[...] = jnp.zeros_like(sums)
+
+    def denormalise(i, carry):
+        rows = pl.ds(pl.multiple_of(i * STEP, STEP), STEP)
+        du = du_ref[rows, :]
+        n = n_ref[rows, :]
+        sums[0:1, :] += jnp.sum(du * n, axis=0, keepdims=True)
+        sums[1:2, :] += jnp.sum(du, axis=0, keepdims=True)
+        e = du * gain[...]
+        e_mean = jnp.mean(e, axis=-1, keepdims=True)
+        en_mean = jnp.mean(e * n, axis=-1, keepdims=True)
+        dh_ref[rows, :] = (inv_ref[rows, 0:1] * (e - e_mean - n * en_mean)).astype(BF)
+        return carry
+
+    lax.fori_loop(0, ROWS // STEP, denormalise, 0)
+    small[2 * half + 1 : 2 * half + 3, :] = sums[0:2, :]
+
+    def lin_grad(i, carry):
+        cols = pl.ds(pl.multiple_of(i * 256, 256), 256)
+        g_lin[:, cols] = mm_tn(a3[...], dh_ref[:, cols])
+        return carry
+
+    lax.fori_loop(0, width // 256, lin_grad, 0)
+
+    def later(v):
+        return pltpu.roll(v.astype(F32), ROWS - 1, 0)
+
+    ez3 = through_silu(mm_nt(dh_ref[...], lin[...]), z3[...])
+    three[256:, :] = mm_tn(a2[...], ez3)
+    three[:256, :] = mm_tn(a2[:, 256:], later(ez3).astype(BF))
+    first = through_silu(mm_nt(ez3, w_three[256:512, :]), z2[:, :256])
+    over = later(mm_nt(ez3, w_three[:256, :]))
+    second = through_silu(mm_nt(ez3, w_three[512:, :]) + over, z2[:, 256:])
+    side = mm_tn(a1[:, 256:], second)
+    two[:256, :] = mm_tn(a1[:, 768:], later(first).astype(BF)) + side[:256]
+    two[256:, :] = mm_tn(a1[:, :512], first) + side[256:]
+    da = (
+        mm_nt(first, w_two[256:512, :]),
+        mm_nt(first, w_two[512:, :]) + mm_nt(second, w_two[:256, :]),
+        mm_nt(second, w_two[256:512, :]),
+        mm_nt(second, w_two[512:, :]) + later(mm_nt(first, w_two[:256, :])),
+    )
+    tops = (0, 80, 112, 16)
+    total = None
+    for j in (1, 2, 3):
+        low, high = windows[j]
+        ez = through_silu(da[j], z1[:, 256 * j : 256 * j + 256])
+        term = mm_tn(xw[:, low:high], ez)[tops[j] : tops[j] + 240]
+        total = term if total is None else total + term
+    ez = through_silu(da[0], z1[:, :256])
+    here = mm_tn(xw[:, :256], ez)[:160]
+    gone = mm_tn(xw[:, 640:768], ez)[48:]
+    one[...] = total + jnp.concatenate([gone, here], axis=0)
+    for copy in started:
+        copy.wait_send()
+
+
+def work(live, mel, cot, proj, w_one, w_two, w_three, lin, gain, bias, taps, tm_n, half, scale):
+    width = lin.shape[1]
+    vmem = pl.BlockSpec(memory_space=pltpu.VMEM)
+    ny = tm_n // CORES
+    copies = 2 + 2 * (ny - 1) + 1
+
+    def buf(*shape, dtype=BF):
+        return pltpu.VMEM(shape, dtype)
+
+    return pl.pallas_call(
+        functools.partial(work_kernel, tm_n, half, scale),
+        out_shape=[
+            jax.ShapeDtypeStruct(shape, F32)
+            for shape in ((240, 256), (768, 256), (768, 256), (256, width), (16, width))
+        ],
+        in_specs=[pl.BlockSpec(memory_space=pltpu.SMEM)] + [vmem] * 10,
+        out_specs=[vmem] * 5,
+        scratch_shapes=[
+            buf(tm_n, *proj.shape),
+            buf(ROWS, 768),
+            buf(RIM, 640),
+            buf(RIM, 640),
+            buf(RIM, 640),
+            buf(ROWS, 1024, dtype=F32),
+            buf(ROWS, 512, dtype=F32),
+            buf(ROWS, 256, dtype=F32),
+            buf(ROWS, 1024),
+            buf(ROWS, 512),
+            buf(ROWS, 256),
+            buf(ROWS, width, dtype=F32),
+            buf(ROWS, 128, dtype=F32),
+            buf(ROWS, width),
+            buf(ROWS, width, dtype=F32),
+            buf(ROWS, width),
+            buf(ROWS, width, dtype=F32),
+            buf(tm_n, ROWS, 256),
+            buf(ROWS, width),
+            buf(8, width, dtype=F32),
+            pltpu.SemaphoreType.DMA,
+            pltpu.SemaphoreType.DMA((copies,)),
+            pltpu.SemaphoreType.DMA((copies,)),
+        ],
+        compiler_params=pltpu.CompilerParams(
+            collective_id=1, has_side_effects=True, vmem_limit_bytes=56 * 1024 * 1024
+        ),
+    )(live, mel, cot, proj, w_one, w_two, w_three, lin, gain, bias, taps)
+
+
 def per_device(
     mel,
     cotangent,
@@ -285,111 +559,28 @@
     blocks,
 ):
     tm_count = lax.axis_size("tm")
-    tm_rank = lax.axis_index("tm")
     dp_count = lax.axis_size("dp")
-    rows_dev = mel.shape[1]
-    bins = conv_one.shape[0] // 3
-    ch = conv_two.shape[1]
-    width = linear_weight.shape[1]
+    block_rows = mel.shape[1] // dp_count
     taps = dw_kernel.shape[0]
-    half = taps // 2
-    rows = rows_dev + 16
-    total_blocks = (dp_count * dp_count + 2) // 3
-    block_rows = rows_dev // dp_count
-    live = blocks[lax.axis_index("dp")] * block_rows
-    scale = lax.rsqrt(F32(total_blocks * block_rows * tm_count))
-
-    proj_full = lax.all_gather(proj, "tm", axis=1, tiled=True)
-    up = [(i, i + 1) for i in range(tm_count - 1)]
-    down = [(i + 1, i) for i in range(tm_count - 1)]
-    tail = lax.dynamic_slice_in_dim(mel[0], live - half - 1, half + 1, 0)
-    before = lax.ppermute(tail, "tm", up)
-    after = lax.ppermute(mel[0, :half], "tm", down)
-    ids = jnp.arange(rows, dtype=jnp.int32)[:, None]
-    own = ids < live
-    x = jnp.where(own, jnp.pad(mel[0], ((0, rows - rows_dev), (0, 0))), jnp.zeros((), BF))
-    x = lax.dynamic_update_slice(x, after, (live, 0))
-    x = lax.dynamic_update_slice(x, before, (rows - half - 1, 0))
-    valid = (
-        own
-        | ((ids < live + half) & (tm_rank < tm_count - 1))
-        | ((ids >= rows - half) & (tm_rank > 0))
+    total_rows = (dp_count * dp_count + 2) // 3 * block_rows * tm_count
+    live = (blocks[lax.axis_index("dp")] * block_rows)[None]
+    results = work(
+        live,
+        mel[0],
+        cotangent[0],
+        proj,
+        wide_conv_one(conv_one),
+        conv_two,
+        conv_three,
+        linear_weight,
+        ln_gain[None],
+        ln_bias[None],
+        jnp.pad(dw_kernel.astype(F32), ((0, 16 - taps), (0, 0))),
+        tm_count,
+        taps // 2,
+        total_rows**-0.5,
     )
-    cot = jnp.where(own, jnp.pad(cotangent[0], ((0, rows - rows_dev), (0, 0))), jnp.zeros((), BF))
-
-    x_wide = jnp.concatenate([x, roll(x[:, 7 * bins :], 1)], axis=1)
-    w_one = wide_conv_one(conv_one)
-    z1 = mm(x_wide, w_one)
-    a1 = silu(z1)
-    z2 = jnp.concatenate(
-        [
-            mm(a1[:, : 2 * ch], conv_two[ch:]) + mm(roll(a1[:, 3 * ch :], 1), conv_two[:ch]),
-            mm(a1[:, ch:], conv_two),
-        ],
-        axis=1,
-    )
-    a2 = silu(z2)
-    z3 = mm(a2, conv_three[ch:]) + mm(roll(a2[:, ch:], 1), conv_three[:ch])
-    a3 = silu(z3)
-    h = mm(a3, linear_weight).astype(BF).astype(F32)
-    centred = h - jnp.mean(h, axis=-1, keepdims=True)
-    inverse = lax.rsqrt(jnp.mean(jnp.square(centred), axis=-1, keepdims=True) + EPSILON)
-    n = centred * inverse
-    u = (n * ln_gain + ln_bias).astype(BF)
-    m = mm(u, proj_full)
-    value = m[:, :width]
-    gate = jax.nn.sigmoid(m[:, width:])
-    gated = jnp.where(valid, (value * gate).astype(BF).astype(F32), 0.0)
-
-    c = cot.astype(F32) * scale
-    kernel_float = dw_kernel.astype(F32)
-    grad_kernel = []
-    eg = jnp.zeros((rows, width), F32)
-    for k in range(taps):
-        grad_kernel.append(jnp.sum(c * roll(gated, half - k), axis=0))
-        eg = eg + roll(c, k - half) * kernel_float[k]
-    grad_kernel = jnp.stack(grad_kernel, axis=0)
-    eg = jnp.where(valid, eg, 0.0).astype(BF).astype(F32)
-
-    value_grad = eg * gate
-    gate_grad = value_grad * value * (1.0 - gate)
-    em = jnp.concatenate([value_grad, gate_grad], axis=1).astype(BF)
-    du = mm_nt(em, proj_full)
-    grad_gain = jnp.sum(du * n, axis=0)
-    grad_bias = jnp.sum(du, axis=0)
-    e = du * ln_gain
-    dh = (
-        inverse
-        * (e - jnp.mean(e, axis=-1, keepdims=True) - n * jnp.mean(e * n, axis=-1, keepdims=True))
-    ).astype(BF)
-    grad_lin = mm_tn(a3, dh)
-    ez3 = through_silu(mm_nt(dh, linear_weight), z3)
-    ez3_next = roll(ez3, -1)
-    grad_three = jnp.concatenate([mm_tn(a2[:, ch:], ez3_next), mm_tn(a2, ez3)], axis=0)
-    da2 = mm_nt(ez3, conv_three[ch:])
-    da2 = jnp.concatenate([da2[:, :ch], da2[:, ch:] + mm_nt(ez3_next, conv_three[:ch])], axis=1)
-    ez2 = through_silu(da2, z2)
-    first, second = ez2[:, :ch], ez2[:, ch:]
-    first_next = roll(first, -1)
-    grad_two = (
-        jnp.concatenate([mm_tn(a1[:, 3 * ch :], first_next), mm_tn(a1[:, : 2 * ch], first)], axis=0)
-        + mm_tn(a1[:, ch:], second)
-    )
-    left = mm_nt(first, conv_two[ch:])
-    right = mm_nt(second, conv_two)
-    over = mm_nt(first_next, conv_two[:ch])
-    da1 = jnp.concatenate(
-        [left[:, :ch], left[:, ch:] + right[:, :ch], right[:, ch : 2 * ch], right[:, 2 * ch :] + over],
-        axis=1,
-    )
-    ez1 = through_silu(da1, z1)
-    grad_one = narrow_conv_one(mm_tn(x_wide, ez1))
-    small = jnp.concatenate(
-        [grad_kernel, grad_gain[None], grad_bias[None], jnp.zeros((16 - taps - 2, width), F32)], axis=0
-    )
-    one, two, three, lin, small = sum_everywhere(
-        (grad_one, grad_two, grad_three, grad_lin, small), dp_count // NX, tm_count // CORES
-    )
+    one, two, three, lin, small = sum_everywhere(results, dp_count // NX, tm_count // CORES)
     return (one, two, three, lin, small[taps], small[taps + 1], small[:taps])
 
 

time: 172 us -> 130 us (0.76)
  Pallas kernels: 62.4 us -> 112 us
  waiting for transfers between devices: 22.7 us -> 0 us
  local copies, waits for them, and re-layouts: 28.1 us -> 10.9 us
  matrix products: 16.7 us -> 0 us
  between operations: 15.5 us -> 1.33 us
  starting transfers between devices: 10.7 us -> 0 us
  other arithmetic: 15.2 us -> 5.38 us
    pallas_call x0 -> x1, Pallas kernels: none -> 51.6 us  [work(): pl.pallas_call(functools.partial(work_kernel, tm_n, half, scale), out_sha...]
    all_gather x1 -> x0, waiting for transfers between devices: 22 us -> none  [per_device(): proj_full = lax.all_gather(proj, 'tm', axis=1, tiled=True)]
    dot_general x22 -> x0, matrix products: 16.7 us -> none  [the longest x8 7.77 us: mm(): return jnp.dot(lhs, rhs, preferred_element_type=F32)]
    ppermute x2 -> x0, starting transfers between devices: 10.6 us -> none  [the longest x1 8.73 us: per_device(): after = lax.ppermute(mel[0, :half], 'tm', down)]
    slice x30 -> x0, local copies, waits for them, and re-layouts: 8.53 us -> none  [the longest x26 8.46 us: roll(): return jnp.roll(values, shift, axis=0)]
    unnamed x71 -> x9, local copies, waits for them, and re-layouts: 13.8 us -> 6.5 us
    another operation x1 -> x0, other arithmetic: 4.95 us -> none
    reduce_sum x3 -> x0, other arithmetic: 4.69 us -> none  [the longest x2 4.35 us: per_device(): grad_kernel.append(jnp.sum(c * roll(gated, half - k), axis=0))]
  transfers between devices with their start and end apart: 3 -> 0, of which waited for: 1 -> 0; matrix products, arithmetic and copies ran while one was open for 10% -> 0% of each run, Pallas kernels for 0% -> 0%
where the time goes in v3:
time: 130 us; the launch traced here: 129 us
  Pallas kernels  112 us (86%)
  local copies, waits for them, and re-layouts  10.9 us (8%)
  other arithmetic  5.38 us (4%)
  between operations  1.33 us (1%)
    pallas_call x1, Pallas kernels, sum_everywhere(): pl.pallas_call(functools.partial(sum_kernel, nz, ny), out_shape=[jax.Shap...  60.2 us
    pallas_call x1, Pallas kernels, work(): pl.pallas_call(functools.partial(work_kernel, tm_n, half, scale), out_sha...  51.6 us
    unnamed x9, local copies, waits for them, and re-layouts  6.5 us
    concatenate x1, other arithmetic, wide_conv_one(): return jnp.concatenate(columns, axis=1)  3.99 us

profile of v3, /device:TPU:1, one launch (start us, length us, event | category | flops | bytes accessed | tf_op | source)
XLA Modules:
  0.0 129.4 jit_solution(462209738877054837)
XLA Ops:
  0.6 1.2 dynamic_slice.3
  2.5 0.8 slice.16
  3.3 1.4 %pad_convert_fusion.taps = f32[16,1024]{1,0:T(8,128)} fusion(bf16[9,1024]{1,0:T(8,128)(2,1)} %param.20), kind=kLoop, calls=%fused_computation.13 | loop fusion | flops 16384 | bytes 83968 | tf_op jit(solution)/shard_map/jit(_pad)/pad | solution.py:578
  4.7 0.9 slice.15
  5.6 4.0 %fusion.6.w_one = bf16[768,1024]{1,0:T(8,128)(2,1)} fusion(bf16[240,256]{1,0:T(8,128)(2,1)} %param.13, bf16[80,256]{1,0:T(8,128)(2,1)S(1)} %slice.16, bf16[528,256]{1,0:T(8,128)(2,1)S(1)} %broadcast_in_dim.10, bf16[160,256]{1,0:T(8,128)(2,1)S(1)} %slice.15), kind=kLoop, calls=%fused_computation.11 | loop fusion | flops 17301504 | bytes 2088960 | tf_op jit(solution)/shard_map/concatenate | solution.py:47
  9.6 51.6 %shard_map.162 = (f32[240,256]{1,0:T(8,128)}, f32[768,256]{1,0:T(8,128)}, f32[768,256]{1,0:T(8,128)}, f32[256,1024]{1,0:T(8,128)}, f32[16,1024]{1,0:T(8,128)}) custom-call(s32[1]{0:T(128)S(6)} %mul.4.live_ref, bf16[320,640]{1,0:T(8,128)(2,1)} %bitcast.6, bf16[320,1024]{1,0:T(8,128)(2,1)} %bitcast.5, bf16[1024,256]{1,0:T(8,128)(2,1)} %proj.1, ...), custom_call_target="tpu_custom_call" | custom-call | tf_op jit(solution)/shard_map/pallas_call | solution.py:509
  61.2 60.2 %shard_map.163 = (bf16[240,256]{1,0:T(8,128)(2,1)}, bf16[768,256]{1,0:T(8,128)(2,1)}, bf16[768,256]{1,0:T(8,128)(2,1)}, bf16[256,1024]{1,0:T(8,128)(2,1)}, bf16[16,1024]{1,0:T(8,128)(2,1)}) custom-call(f32[240,256]{1,0:T(8,128)} %get-tuple-element.17.one, f32[768,256]{1,0:T(8,128)} %get-tuple-element.18.two, f32[768,256]{1,0:T(8,128)} %get-tuple-element.19.three, ...), custom_call_target="tpu_custom_call" | custom-call | tf_op jit(solution)/shard_map/pallas_call | solution.py:236
  121.5 0.0 copy-start
  121.5 0.0 copy-start.1
  121.5 1.4 %slice_reduce_fusion = (bf16[1024]{0:T(1024)(128)(2,1)}, bf16[1024]{0:T(1024)(128)(2,1)}) fusion(bf16[16,1024]{1,0:T(8,128)(2,1)} %get-tuple-element.26), kind=kLoop, calls=%fused_computation.14 | loop fusion | bytes 8192 | tf_op jit(solution)/shard_map/slice | solution.py:584
  122.9 1.6 %copy.23 = bf16[240,256]{1,0:T(8,128)(2,1)} copy(bf16[240,256]{1,0:T(8,128)(2,1)} %get-tuple-element.36) | data formatting | bytes 245760
  124.5 1.8 %copy.24 = bf16[768,256]{1,0:T(8,128)(2,1)} copy(bf16[768,256]{1,0:T(8,128)(2,1)} %get-tuple-element.37) | data formatting | bytes 786432
  126.3 1.8 %copy.25 = bf16[768,256]{1,0:T(8,128)(2,1)} copy(bf16[768,256]{1,0:T(8,128)(2,1)} %get-tuple-element.38) | data formatting | bytes 786432
  128.0 0.0 copy-done
  128.0 0.8 copy.26
  128.8 0.0 copy-done.1
  128.8 0.6 copy.27
  (1 shorter events, 0.0 us)
Async XLA Ops:
  121.5 6.5 %copy-start = (bf16[256,1024]{1,0:T(8,128)(2,1)S(1)}, bf16[256,1024]{1,0:T(8,128)(2,1)}, u32[]{:S(2)}) copy-start(bf16[256,1024]{1,0:T(8,128)(2,1)} %get-tuple-element.39) | copy-start | bytes 1572868
  121.5 7.3 %copy-start.1 = (bf16[16,1024]{1,0:T(8,128)(2,1)S(1)}, bf16[16,1024]{1,0:T(8,128)(2,1)}, u32[]{:S(2)}) copy-start(bf16[16,1024]{1,0:T(8,128)(2,1)} %get-tuple-element.26) | copy-start | bytes 98308

commit v4 on v3

--- a/solution.py
+++ b/solution.py
@@ -33,23 +33,9 @@
     return (grad * (s * (1.0 + z * (1.0 - s)))).astype(BF)
 
 
-def wide_conv_one(conv):
-    bins, ch = conv.shape[0] // 3, conv.shape[1]
-    rows = 768
-
-    def zeros(count):
-        return jnp.zeros((count, ch), conv.dtype)
-
-    columns = [jnp.concatenate([conv[bins:], zeros(rows - 3 * bins), conv[:bins]], axis=0)]
-    for slot in range(1, 4):
-        top = (2 * slot - 1) * bins
-        columns.append(jnp.pad(conv, ((top, rows - top - 3 * bins), (0, 0))))
-    return jnp.concatenate(columns, axis=1)
-
-
 NX = 4
 CORES = 2
-PIECE = 96
+PIECE = 48
 LANES = 256
 SUB = 8
 
@@ -59,17 +45,16 @@
 
 
 def sum_kernel(
-    nz, ny, one, two, three, lin, small, o_one, o_two, o_three, o_lin, o_small,
-    acc, out, snd, from_core, from_y, from_x, z_acc, z_snd, from_z, z_out, send_sem, recv_sem,
+    nz, ny, one, two, three, lin, small, result,
+    acc, out, snd, from_core, from_first, from_second, z_acc, z_snd, from_z, z_out,
+    send_sem, recv_sem,
 ):
     dp, tm = lax.axis_index("dp"), lax.axis_index("tm")
     z, x = dp // NX, dp % NX
     y, core = tm // CORES, tm % CORES
-    chunk = NX * PIECE
-    half = ny * chunk
-
-    def at_core():
-        return (dp, y * CORES + (1 - core))
+    fan = NX
+    chunk = fan * PIECE
+    half = fan * chunk
 
     def at_y(d):
         return (dp, ((y + d) % ny) * CORES + core)
@@ -80,27 +65,27 @@
     def at_z(d):
         return (((z + d) % nz) * NX + x, tm)
 
+    at_core = (dp, y * CORES + (1 - core))
+    colours = ((0, y, at_y, x, at_x), (1, x, at_x, y, at_y))
+
     barrier = pltpu.get_barrier_semaphore()
     peers = [at_z(d) for d in range(1, nz)] + [at_x(d) for d in range(1, NX)]
-    peers = peers + [at_y(d) for d in range(1, ny)] + [at_core()]
+    peers = peers + [at_y(d) for d in range(1, ny)] + [at_core]
     for peer in peers:
         pl.semaphore_signal(barrier, inc=1, device_id=peer, device_id_type=pl.DeviceIdType.MESH)
 
-    first = 0
-    places = []
-    for src, dst in ((one, o_one), (two, o_two), (three, o_three), (lin, o_lin), (small, o_small)):
+    top = 0
+    for src in (one, two, three, lin, small):
         for lane in range(0, src.shape[1], LANES):
-            places.append((src, dst, lane, first, src.shape[0]))
-            first += src.shape[0]
-    for src, _, lane, top, count in places:
-        step = 16 if count % 48 else 48
-
-        def fill(i, src=src, lane=lane, top=top, step=step):
-            acc[pl.ds(top + i, step), :] = src[pl.ds(i, step), pl.ds(lane, LANES)]
-
-        row_loop(count, step, fill)
-    rest = acc.shape[0] - first
-    acc[pl.ds(first, rest), :] = jnp.zeros((rest, LANES), F32)
+            step = 16 if src.shape[0] % 48 else 48
+
+            def fill(i, src=src, lane=lane, top=top, step=step):
+                acc[pl.ds(top + i, step), :] = src[pl.ds(i, step), pl.ds(lane, LANES)]
+
+            row_loop(src.shape[0], step, fill)
+            top += src.shape[0]
+    rest = acc.shape[0] - top
+    acc[pl.ds(top, rest), :] = jnp.zeros((rest, LANES), F32)
 
     started = []
 
@@ -118,79 +103,86 @@
         started.append(copy)
         return copy
 
-    mine = core * half
-    theirs = (1 - core) * half
-    order = list(range(1, ny)) + [0]
+    def mine(colour):
+        return (colour * CORES + core) * half
+
+    def theirs(colour):
+        return (colour * CORES + 1 - core) * half
+
+    order = list(range(1, fan)) + [0]
     pl.semaphore_wait(barrier, len(peers))
     core_copies = []
     for d in order:
-        place = pl.multiple_of(((y + d) % ny) * chunk, PIECE)
-
-        def narrow(i, place=place):
-            at = pl.multiple_of(theirs + place + i, 48)
-            snd[pl.ds(at, 48), :] = acc[pl.ds(at, 48), :].astype(BF)
-
-        row_loop(chunk, 48, narrow)
-        core_copies.append(
-            send(
-                snd.at[pl.ds(pl.multiple_of(theirs + place, PIECE), chunk)],
-                from_core.at[pl.ds(place, chunk)],
-                at_core(),
-            )
-        )
-    y_copies = []
-    for d, copy in zip(order, core_copies):
-        copy.wait_recv()
-        place = pl.multiple_of(((y + d) % ny) * chunk, PIECE)
-
-        def add_core(i, place=place, d=d):
-            at = pl.multiple_of(mine + place + i, 48)
-            total = acc[pl.ds(at, 48), :] + from_core[
-                pl.ds(pl.multiple_of(place + i, 48), 48), :
-            ].astype(F32)
-            if d == 0:
-                acc[pl.ds(at, 48), :] = total
-            else:
-                snd[pl.ds(at, 48), :] = total.astype(BF)
-
-        row_loop(chunk, 48, add_core)
-        if d:
-            y_copies.append(
+        for colour, first, _, _, _ in colours:
+            place = ((first + d) % fan) * chunk
+
+            def narrow(i, place=place, colour=colour):
+                at = pl.multiple_of(theirs(colour) + place + i, PIECE)
+                snd[pl.ds(at, PIECE), :] = acc[pl.ds(at, PIECE), :].astype(BF)
+
+            row_loop(chunk, PIECE, narrow)
+            core_copies.append(
                 send(
-                    snd.at[pl.ds(pl.multiple_of(mine + place, PIECE), chunk)],
-                    from_y.at[d - 1],
-                    at_y(d),
+                    snd.at[pl.ds(pl.multiple_of(theirs(colour) + place, PIECE), chunk)],
+                    from_core.at[pl.ds(pl.multiple_of(colour * half + place, PIECE), chunk)],
+                    at_core,
                 )
             )
-    for copy in y_copies:
+    first_copies = []
+    for d in order:
+        for colour, first, at_first, _, _ in colours:
+            core_copies.pop(0).wait_recv()
+            place = ((first + d) % fan) * chunk
+
+            def add_core(i, place=place, d=d, colour=colour):
+                at = pl.multiple_of(mine(colour) + place + i, PIECE)
+                came = from_core[pl.ds(pl.multiple_of(colour * half + place + i, PIECE), PIECE), :]
+                total = acc[pl.ds(at, PIECE), :] + came.astype(F32)
+                if d == 0:
+                    acc[pl.ds(at, PIECE), :] = total
+                else:
+                    snd[pl.ds(at, PIECE), :] = total.astype(BF)
+
+            row_loop(chunk, PIECE, add_core)
+            if d:
+                at = pl.multiple_of(mine(colour) + place, PIECE)
+                first_copies.append(
+                    send(snd.at[pl.ds(at, chunk)], from_first.at[colour, d - 1], at_first(d))
+                )
+    for copy in first_copies:
         copy.wait_recv()
-    own = pl.multiple_of(mine + y * chunk, PIECE)
-
-    def add_y(i):
-        at = pl.multiple_of(own + i, 48)
-        total = acc[pl.ds(at, 48), :]
-        for d in range(1, ny):
-            total = total + from_y[d - 1, pl.ds(i, 48), :].astype(F32)
-        acc[pl.ds(at, 48), :] = total
-        snd[pl.ds(at, 48), :] = total.astype(BF)
-
-    row_loop(chunk, 48, add_y)
-    x_copies = []
-    for d in range(1, NX):
-        place = pl.multiple_of(own + ((x + d) % NX) * PIECE, PIECE)
-        x_copies.append(send(snd.at[pl.ds(place, PIECE)], from_x.at[d - 1], at_x(d)))
-    for copy in x_copies:
-        copy.wait_recv()
-    piece = pl.multiple_of(own + x * PIECE, PIECE)
-    total = acc[pl.ds(piece, PIECE), :]
-    for d in range(1, NX):
-        total = total + from_x[d - 1].astype(F32)
+    second_copies = []
+    for colour, first, _, second, at_second in colours:
+        own = mine(colour) + first * chunk
+
+        def add_first(i, own=own, colour=colour):
+            at = pl.multiple_of(own + i, PIECE)
+            total = acc[pl.ds(at, PIECE), :]
+            for d in range(1, fan):
+                total = total + from_first[colour, d - 1, pl.ds(i, PIECE), :].astype(F32)
+            acc[pl.ds(at, PIECE), :] = total
+            snd[pl.ds(at, PIECE), :] = total.astype(BF)
+
+        row_loop(chunk, PIECE, add_first)
+        for d in range(1, fan):
+            at = pl.multiple_of(own + ((second + d) % fan) * PIECE, PIECE)
+            second_copies.append(
+                send(snd.at[pl.ds(at, PIECE)], from_second.at[colour, d - 1], at_second(d))
+            )
     parts = PIECE // SUB
-    total = total.reshape(parts, SUB, LANES)
-    z_acc[pl.ds(0, parts)] = total
-    z_snd[pl.ds(0, parts)] = total.astype(BF)
-    z_acc[pl.ds(parts, nz - parts)] = jnp.zeros((nz - parts, SUB, LANES), F32)
-    z_snd[pl.ds(parts, nz - parts)] = jnp.zeros((nz - parts, SUB, LANES), BF)
+    for colour, first, _, second, _ in colours:
+        for _ in range(1, fan):
+            second_copies.pop(0).wait_recv()
+        piece = pl.multiple_of(mine(colour) + first * chunk + second * PIECE, PIECE)
+        total = acc[pl.ds(piece, PIECE), :]
+        for d in range(1, fan):
+            total = total + from_second[colour, d - 1].astype(F32)
+        total = total.reshape(parts, SUB, LANES)
+        z_acc[pl.ds(colour * parts, parts)] = total
+        z_snd[pl.ds(colour * parts, parts)] = total.astype(BF)
+    used = 2 * parts
+    z_acc[pl.ds(used, nz - used)] = jnp.zeros((nz - used, SUB, LANES), F32)
+    z_snd[pl.ds(used, nz - used)] = jnp.zeros((nz - used, SUB, LANES), BF)
     far = sorted(range(1, nz), key=lambda d: -min(d, nz - d))
     z_copies = [send(z_snd.at[(z + d) % nz], from_z.at[d - 1], at_z(d)) for d in far]
     for copy in z_copies:
@@ -202,49 +194,65 @@
     z_copies = [send(z_out.at[z], z_out.at[z], at_z(d)) for d in far]
     for copy in z_copies:
         copy.wait_recv()
-    done = z_out[pl.ds(0, parts)].astype(F32).reshape(PIECE, LANES)
-    out[pl.ds(piece, PIECE), :] = done.astype(BF)
-    whole = out.at[pl.ds(piece, PIECE)]
-    x_copies = [send(whole, whole, at_x(d)) for d in range(1, NX)]
-    for copy in x_copies:
+    for colour, first, _, second, at_second in colours:
+        done = z_out[pl.ds(colour * parts, parts)].astype(F32).reshape(PIECE, LANES)
+        piece = pl.multiple_of(mine(colour) + first * chunk + second * PIECE, PIECE)
+        out[pl.ds(piece, PIECE), :] = done.astype(BF)
+        whole = out.at[pl.ds(piece, PIECE)]
+        second_copies.extend([send(whole, whole, at_second(d)) for d in range(1, fan)])
+    for copy in second_copies:
         copy.wait_recv()
-    whole = out.at[pl.ds(own, chunk)]
-    y_copies = [send(whole, whole, at_y(d)) for d in range(1, ny)]
-    core_copies = [send(whole, whole, at_core())]
-    for d, copy in zip(range(1, ny), y_copies):
-        copy.wait_recv()
-        place = pl.multiple_of(mine + ((y - d + ny) % ny) * chunk, PIECE)
-        whole = out.at[pl.ds(place, chunk)]
-        core_copies.append(send(whole, whole, at_core()))
+    first_copies = []
+    for colour, first, at_first, _, _ in colours:
+        whole = out.at[pl.ds(pl.multiple_of(mine(colour) + first * chunk, PIECE), chunk)]
+        first_copies.append([send(whole, whole, at_first(d)) for d in range(1, fan)])
+        core_copies.append(send(whole, whole, at_core))
+    for d in range(1, fan):
+        for colour, first, _, _, _ in colours:
+            first_copies[colour][d - 1].wait_recv()
+            place = pl.multiple_of(mine(colour) + ((first - d + fan) % fan) * chunk, PIECE)
+            whole = out.at[pl.ds(place, chunk)]
+            core_copies.append(send(whole, whole, at_core))
     for copy in core_copies:
         copy.wait_recv()
+
+    def drain(i):
+        result[pl.ds(i, PIECE), :] = out[pl.ds(i, PIECE), :]
+
+    row_loop(out.shape[0], PIECE, drain)
     for copy in started:
         copy.wait_send()
-    for _, dst, lane, top, count in places:
-        step = 16 if count % 48 else 48
-
-        def drain(i, dst=dst, lane=lane, top=top, step=step):
-            dst[pl.ds(i, step), pl.ds(lane, LANES)] = out[pl.ds(top + i, step), :]
-
-        row_loop(count, step, drain)
+
+
+def unpack_kernel(packed, one, two, three, lin, small):
+    top = 0
+    for dst in (one, two, three, lin, small):
+        for lane in range(0, dst.shape[1], LANES):
+            step = 16 if dst.shape[0] % 48 else 48
+
+            def drain(i, dst=dst, lane=lane, top=top, step=step):
+                dst[pl.ds(i, step), pl.ds(lane, LANES)] = packed[pl.ds(top + i, step), :]
+
+            row_loop(dst.shape[0], step, drain)
+            top += dst.shape[0]
 
 
 def sum_everywhere(pieces, nz, ny):
-    total = CORES * ny * NX * PIECE
-    copies = 2 * (ny + (ny - 1) + (NX - 1) + (nz - 1))
+    total = 2 * CORES * NX * NX * PIECE
+    copies = 2 * (2 * (NX + 2 * (NX - 1)) + nz - 1)
     vmem = pl.BlockSpec(memory_space=pltpu.VMEM)
-    return pl.pallas_call(
+    packed = pl.pallas_call(
         functools.partial(sum_kernel, nz, ny),
-        out_shape=[jax.ShapeDtypeStruct(p.shape, BF) for p in pieces],
+        out_shape=jax.ShapeDtypeStruct((total, LANES), BF),
         in_specs=[vmem] * len(pieces),
-        out_specs=[vmem] * len(pieces),
+        out_specs=vmem,
         scratch_shapes=[
             pltpu.VMEM((total, LANES), F32),
             pltpu.VMEM((total, LANES), BF),
             pltpu.VMEM((total, LANES), BF),
             pltpu.VMEM((total // CORES, LANES), BF),
-            pltpu.VMEM((ny - 1, NX * PIECE, LANES), BF),
-            pltpu.VMEM((NX - 1, PIECE, LANES), BF),
+            pltpu.VMEM((2, NX - 1, NX * PIECE, LANES), BF),
+            pltpu.VMEM((2, NX - 1, PIECE, LANES), BF),
             pltpu.VMEM((nz, SUB, LANES), F32),
             pltpu.VMEM((nz, SUB, LANES), BF),
             pltpu.VMEM((nz - 1, SUB, LANES), BF),
@@ -254,6 +262,12 @@
         ],
         compiler_params=pltpu.CompilerParams(collective_id=0, has_side_effects=True),
     )(*pieces)
+    return pl.pallas_call(
+        unpack_kernel,
+        out_shape=[jax.ShapeDtypeStruct(p.shape, BF) for p in pieces],
+        in_specs=[vmem],
+        out_specs=[vmem] * len(pieces),
+    )(packed)
 
 
 ROWS = 336
@@ -262,17 +276,18 @@
 
 
 def work_kernel(
-    tm_n, half, scale, live_ref, mel, cot, proj, w_one, w_two, w_three, lin, gain, bias, taps,
+    tm_n, half, block_rows, scale, blocks, mel_ref, cot_ref, proj, conv_one, w_two, w_three, lin, gain, bias, taps,
     one, two, three, g_lin, small,
-    full, xw, up_snd, up_rcv, down_rcv, z1, z2, z3, a1, a2, a3, n_ref, inv_ref, u_ref, du_ref,
+    full, w_one, xw, up_snd, up_rcv, down_rcv, z1, z2, z3, a1, a2, a3, n_ref, inv_ref, u_ref, du_ref,
     eg_ref, gated_ref, em, dh_ref, sums, own_sem, send_sem, recv_sem,
 ):
     dp, tm = lax.axis_index("dp"), lax.axis_index("tm")
     ny = tm_n // CORES
     y, core = tm // CORES, tm % CORES
+    mel, cot = mel_ref.at[0], cot_ref.at[0]
     own_rows = mel.shape[0]
     width = lin.shape[1]
-    live = live_ref[0]
+    live = blocks[dp] * block_rows
 
     def at(d):
         return (dp, (tm + d) % tm_n)
@@ -285,6 +300,17 @@
     column = lax.broadcasted_iota(jnp.int32, (RIM, own_rows), 1)
     pick = (column - live == first_row - RIM) & (first_row >= RIM - half - 1)
     up_snd[...] = mm(pick.astype(F32).astype(BF), mel[...]).astype(BF)
+    bins = conv_one.shape[0] // 3
+
+    def clear(i):
+        w_one[pl.ds(i, 48), :] = jnp.zeros((48, 1024), BF)
+
+    row_loop(768, 48, clear)
+    w_one[: 2 * bins, :256] = conv_one[bins:, :]
+    w_one[768 - bins :, :256] = conv_one[:bins, :]
+    for j in range(1, 4):
+        above = (2 * j - 1) * bins
+        w_one[above : above + 3 * bins, 256 * j : 256 * j + 256] = conv_one[...]
     pl.semaphore_wait(barrier, tm_n - 1)
 
     started = []
@@ -327,9 +353,10 @@
         cols = pl.ds(pl.multiple_of(i * 128, 128), 128)
         c = cot_block(cols)
         total = jnp.zeros_like(c)
+        weights = taps[:, cols].astype(F32)
         for k in range(2 * half + 1):
             shifted = pltpu.roll(c, (k - half) % ROWS, 0) if k != half else c
-            total = total + shifted * taps[k : k + 1, cols]
+            total = total + shifted * weights[k : k + 1]
         eg_ref[:, cols] = jnp.where(mask(ROWS, 128), total, 0.0).astype(BF)
         return carry
 
@@ -497,7 +524,8 @@
         copy.wait_send()
 
 
-def work(live, mel, cot, proj, w_one, w_two, w_three, lin, gain, bias, taps, tm_n, half, scale):
+def work(operands, tm_n, half, block_rows, scale):
+    proj, lin = operands[3], operands[7]
     width = lin.shape[1]
     vmem = pl.BlockSpec(memory_space=pltpu.VMEM)
     ny = tm_n // CORES
@@ -507,7 +535,7 @@
         return pltpu.VMEM(shape, dtype)
 
     return pl.pallas_call(
-        functools.partial(work_kernel, tm_n, half, scale),
+        functools.partial(work_kernel, tm_n, half, block_rows, scale),
         out_shape=[
             jax.ShapeDtypeStruct(shape, F32)
             for shape in ((240, 256), (768, 256), (768, 256), (256, width), (16, width))
@@ -516,6 +544,7 @@
         out_specs=[vmem] * 5,
         scratch_shapes=[
             buf(tm_n, *proj.shape),
+            buf(768, 1024),
             buf(ROWS, 768),
             buf(RIM, 640),
             buf(RIM, 640),
@@ -542,7 +571,7 @@
         compiler_params=pltpu.CompilerParams(
             collective_id=1, has_side_effects=True, vmem_limit_bytes=56 * 1024 * 1024
         ),
-    )(live, mel, cot, proj, w_one, w_two, w_three, lin, gain, bias, taps)
+    )(*operands)
 
 
 def per_device(
@@ -563,21 +592,23 @@
     block_rows = mel.shape[1] // dp_count
     taps = dw_kernel.shape[0]
     total_rows = (dp_count * dp_count + 2) // 3 * block_rows * tm_count
-    live = (blocks[lax.axis_index("dp")] * block_rows)[None]
     results = work(
-        live,
-        mel[0],
-        cotangent[0],
-        proj,
-        wide_conv_one(conv_one),
-        conv_two,
-        conv_three,
-        linear_weight,
-        ln_gain[None],
-        ln_bias[None],
-        jnp.pad(dw_kernel.astype(F32), ((0, 16 - taps), (0, 0))),
+        (
+            blocks,
+            mel,
+            cotangent,
+            proj,
+            conv_one,
+            conv_two,
+            conv_three,
+            linear_weight,
+            ln_gain[None],
+            ln_bias[None],
+            dw_kernel,
+        ),
         tm_count,
         taps // 2,
+        block_rows,
         total_rows**-0.5,
     )
     one, two, three, lin, small = sum_everywhere(results, dp_count // NX, tm_count // CORES)

time: 130 us -> 111 us (0.85)
  local copies, waits for them, and re-layouts: 10.9 us -> 1.4 us
  other arithmetic: 5.38 us -> 0 us
  Pallas kernels: 112 us -> 108 us
    unnamed x9 -> x0, local copies, waits for them, and re-layouts: 6.5 us -> none
    concatenate x1 -> x0, other arithmetic: 3.99 us -> none  [wide_conv_one(): return jnp.concatenate(columns, axis=1)]
    pallas_call x2 -> x3, Pallas kernels: 112 us -> 108 us  [the longest x1 53.9 us: sum_everywhere(): pl.pallas_call(functools.partial(sum_kernel, nz, ny), out_shape=jax.Shape...]
    slice x2 -> x0, local copies, waits for them, and re-layouts: 1.68 us -> none  [the longest x1 0.89 us: wide_conv_one(): conv[bins:]]
    pad x1 -> x0, other arithmetic: 1.39 us -> none  [per_device(): jnp.pad(dw_kernel.astype(F32), ((0, 16 - taps), (0, 0)))]
where the time goes in v4:
time: 111 us; the launch traced here: 110 us
  Pallas kernels  108 us (97%)
  local copies, waits for them, and re-layouts  1.4 us (1%)
    pallas_call x1, Pallas kernels, sum_everywhere(): pl.pallas_call(functools.partial(sum_kernel, nz, ny), out_shape=jax.Shape...  53.9 us
    pallas_call x1, Pallas kernels, work(): pl.pallas_call(functools.partial(work_kernel, tm_n, half, block_rows, sca...  51.3 us
    pallas_call x1, Pallas kernels, sum_everywhere(): pl.pallas_call(unpack_kernel, out_shape=[jax.ShapeDtypeStruct(p.shape, BF...  3.17 us

profile of v4, /device:TPU:1, one launch (start us, length us, event | category | flops | bytes accessed | tf_op | source)
XLA Modules:
  0.0 110.4 jit_solution(6446647014855647184)
XLA Ops:
  0.6 51.3 %shard_map.162 = (f32[240,256]{1,0:T(8,128)}, f32[768,256]{1,0:T(8,128)}, f32[768,256]{1,0:T(8,128)}, f32[256,1024]{1,0:T(8,128)}, f32[16,1024]{1,0:T(8,128)}) custom-call(s32[64]{0:T(128)} %blocks.1, bf16[1,320,640]{2,1,0:T(8,128)(2,1)} %mel_ref.1, bf16[1,320,1024]{2,1,0:T(8,128)(2,1)} %cot_ref.1, bf16[1024,256]{1,0:T(8,128)(2,1)} %proj.1, ...), custom_call_target="tpu_custom_call" | custom-call | tf_op jit(solution)/shard_map/pallas_call | solution.py:537
  51.9 53.9 %shard_map.163.packed = bf16[3072,256]{1,0:T(8,128)(2,1)} custom-call(f32[240,256]{1,0:T(8,128)} %get-tuple-element.17.one, f32[768,256]{1,0:T(8,128)} %get-tuple-element.18.two, f32[768,256]{1,0:T(8,128)} %get-tuple-element.19.three, f32[256,1024]{1,0:T(8,128)} %get-tuple-element.20.lin, f32[16,1024]{1,0:T(8,128)} %get-tuple-element.21.small), custom_call_target="tpu_custom_call" | custom-call | tf_op jit(solution)/shard_map/pallas_call | solution.py:244
  105.8 3.2 %shard_map.164 = (bf16[240,256]{1,0:T(8,128)(2,1)}, bf16[768,256]{1,0:T(8,128)(2,1)}, bf16[768,256]{1,0:T(8,128)(2,1)}, bf16[256,1024]{1,0:T(8,128)(2,1)}, bf16[16,1024]{1,0:T(8,128)(2,1)}) custom-call(bf16[3072,256]{1,0:T(8,128)(2,1)} %shard_map.163.packed), custom_call_target="tpu_custom_call" | custom-call | tf_op jit(solution)/shard_map/pallas_call | solution.py:265
  109.0 1.4 %slice_reduce_fusion = (bf16[1024]{0:T(1024)(128)(2,1)}, bf16[1024]{0:T(1024)(128)(2,1)}) fusion(bf16[16,1024]{1,0:T(8,128)(2,1)} %get-tuple-element.26), kind=kLoop, calls=%fused_computation | loop fusion | bytes 8192 | tf_op jit(solution)/shard_map/slice | solution.py:615

commit v5 on v4

--- a/solution.py
+++ b/solution.py
@@ -273,6 +273,9 @@
 ROWS = 336
 STEP = 48
 RIM = 16
+DIRECT = 256
+X_PART = 96
+Z_PART = 192
 
 
 def work_kernel(
@@ -284,6 +287,7 @@
     dp, tm = lax.axis_index("dp"), lax.axis_index("tm")
     ny = tm_n // CORES
     y, core = tm // CORES, tm % CORES
+    depth, x = dp // NX, dp % NX
     mel, cot = mel_ref.at[0], cot_ref.at[0]
     own_rows = mel.shape[0]
     width = lin.shape[1]
@@ -292,9 +296,14 @@
     def at(d):
         return (dp, (tm + d) % tm_n)
 
+    def at_x(d):
+        return (depth * NX + (x + d) % NX, tm)
+
+    at_z = ((depth + 1 - 2 * (depth % 2)) * NX + x, tm)
     barrier = pltpu.get_barrier_semaphore()
-    for d in range(1, tm_n):
-        pl.semaphore_signal(barrier, inc=1, device_id=at(d), device_id_type=pl.DeviceIdType.MESH)
+    peers = [at(d) for d in range(1, tm_n)] + [at_x(d) for d in range(1, NX)] + [at_z]
+    for peer in peers:
+        pl.semaphore_signal(barrier, inc=1, device_id=peer, device_id_type=pl.DeviceIdType.MESH)
 
     first_row = lax.broadcasted_iota(jnp.int32, (RIM, own_rows), 0)
     column = lax.broadcasted_iota(jnp.int32, (RIM, own_rows), 1)
@@ -311,7 +320,7 @@
     for j in range(1, 4):
         above = (2 * j - 1) * bins
         w_one[above : above + 3 * bins, 256 * j : 256 * j + 256] = conv_one[...]
-    pl.semaphore_wait(barrier, tm_n - 1)
+    pl.semaphore_wait(barrier, len(peers))
 
     started = []
 
@@ -332,8 +341,27 @@
     partner = (dp, y * CORES + (1 - core))
     up = send(up_snd, up_rcv, at(1))
     down = send(mel.at[pl.ds(0, RIM)], down_rcv, at(tm_n - 1))
-    y_copies = [(d, send(proj, full.at[tm], (dp, ((y + d) % ny) * CORES + core))) for d in (1, 3, 2)]
+    direct = pl.ds(0, DIRECT)
+
+    def x_part(q):
+        return pl.ds(pl.multiple_of(DIRECT + q * X_PART, 16), X_PART)
+
+    def z_part(q):
+        return pl.ds(pl.multiple_of(DIRECT + NX * X_PART + q * Z_PART, 16), Z_PART)
+
+    def pass_on(came, part, peer):
+        return send(full.at[came, part], full.at[came, part], peer)
+
+    near = (1, 3, 2)
+    y_copies = {}
+    for name, part in (("x", x_part(x)), ("z", z_part(depth % 2)), ("direct", direct)):
+        for d in near:
+            peer = (dp, ((y + d) % ny) * CORES + core)
+            y_copies[name, d] = send(proj.at[part], full.at[tm, part], peer)
     core_copies = [send(proj, full.at[tm], partner)]
+    came = {d: ((y - d + ny) % ny) * CORES + core for d in near}
+    x_copies = {}
+    z_copies = {}
     keep = pltpu.make_async_copy(proj, full.at[tm], own_sem)
     keep.start()
 
@@ -403,6 +431,13 @@
     z3[...] = z
     a3[...] = silu(z)
 
+    for d in near:
+        y_copies["x", d].wait_recv()
+        for far in range(1, NX):
+            x_copies[d, far] = pass_on(came[d], x_part(x), at_x(far))
+    for d in near:
+        core_copies.append(pass_on(came[d], x_part(x), partner))
+
     def project(i, carry):
         cols = pl.ds(pl.multiple_of(i * 256, 256), 256)
         n_ref[:, cols] = mm(a3[...], lin[:, cols]).astype(BF).astype(F32)
@@ -423,10 +458,20 @@
 
     lax.fori_loop(0, ROWS // STEP, normalise, 0)
 
-    for d, copy in y_copies:
-        copy.wait_recv()
-        came = ((y - d + ny) % ny) * CORES + core
-        core_copies.append(send(full.at[came], full.at[came], partner))
+    for d in near:
+        y_copies["z", d].wait_recv()
+        z_copies[d] = pass_on(came[d], z_part(depth % 2), at_z)
+        core_copies.append(pass_on(came[d], z_part(depth % 2), partner))
+    for d in near:
+        y_copies["direct", d].wait_recv()
+        core_copies.append(pass_on(came[d], direct, partner))
+    for d in near:
+        for far in range(1, NX):
+            x_copies[d, far].wait_recv()
+            core_copies.append(pass_on(came[d], x_part((x - far + NX) % NX), partner))
+    for d in near:
+        z_copies[d].wait_recv()
+        core_copies.append(pass_on(came[d], z_part(1 - depth % 2), partner))
     keep.wait()
     for copy in core_copies:
         copy.wait_recv()
@@ -529,7 +574,7 @@
     width = lin.shape[1]
     vmem = pl.BlockSpec(memory_space=pltpu.VMEM)
     ny = tm_n // CORES
-    copies = 2 + 2 * (ny - 1) + 1
+    copies = 3 + (ny - 1) * (3 + (NX - 1) + 1 + 3 + (NX - 1) + 1)
 
     def buf(*shape, dtype=BF):
         return pltpu.VMEM(shape, dtype)

time: 111 us -> 101 us (0.910)
  Pallas kernels: 108 us -> 99.1 us
    pallas_call x1, Pallas kernels: 51.3 us -> 42 us  [work(): pl.pallas_call(functools.partial(work_kernel, tm_n, half, block_rows, sca...]
where the time goes in v5:
time: 101 us
  Pallas kernels  99.1 us (98%)
  local copies, waits for them, and re-layouts  1.4 us (1%)
    pallas_call x1, Pallas kernels, sum_everywhere(): pl.pallas_call(functools.partial(sum_kernel, nz, ny), out_shape=jax.Shape...  53.9 us
    pallas_call x1, Pallas kernels, work(): pl.pallas_call(functools.partial(work_kernel, tm_n, half, block_rows, sca...  42 us
    pallas_call x1, Pallas kernels, sum_everywhere(): pl.pallas_call(unpack_kernel, out_shape=[jax.ShapeDtypeStruct(p.shape, BF...  3.17 us

profile of v5, /device:TPU:1, one launch (start us, length us, event | category | flops | bytes accessed | tf_op | source)
XLA Modules:
  0.0 101.1 jit_solution(5029346029555741954)
XLA Ops:
  0.6 42.0 %shard_map.162 = (f32[240,256]{1,0:T(8,128)}, f32[768,256]{1,0:T(8,128)}, f32[768,256]{1,0:T(8,128)}, f32[256,1024]{1,0:T(8,128)}, f32[16,1024]{1,0:T(8,128)}) custom-call(s32[64]{0:T(128)} %blocks.1, bf16[1,320,640]{2,1,0:T(8,128)(2,1)} %mel_ref.1, bf16[1,320,1024]{2,1,0:T(8,128)(2,1)} %cot_ref.1, bf16[1024,256]{1,0:T(8,128)(2,1)} %proj.1, ...), custom_call_target="tpu_custom_call" | custom-call | tf_op jit(solution)/shard_map/pallas_call | solution.py:582
  42.6 53.9 %shard_map.163.packed = bf16[3072,256]{1,0:T(8,128)(2,1)} custom-call(f32[240,256]{1,0:T(8,128)} %get-tuple-element.17.one, f32[768,256]{1,0:T(8,128)} %get-tuple-element.18.two, f32[768,256]{1,0:T(8,128)} %get-tuple-element.19.three, f32[256,1024]{1,0:T(8,128)} %get-tuple-element.20.lin, f32[16,1024]{1,0:T(8,128)} %get-tuple-element.21.small), custom_call_target="tpu_custom_call" | custom-call | tf_op jit(solution)/shard_map/pallas_call | solution.py:244
  96.6 3.2 %shard_map.164 = (bf16[240,256]{1,0:T(8,128)(2,1)}, bf16[768,256]{1,0:T(8,128)(2,1)}, bf16[768,256]{1,0:T(8,128)(2,1)}, bf16[256,1024]{1,0:T(8,128)(2,1)}, bf16[16,1024]{1,0:T(8,128)(2,1)}) custom-call(bf16[3072,256]{1,0:T(8,128)(2,1)} %shard_map.163.packed), custom_call_target="tpu_custom_call" | custom-call | tf_op jit(solution)/shard_map/pallas_call | solution.py:265
  99.7 1.4 %slice_reduce_fusion = (bf16[1024]{0:T(1024)(128)(2,1)}, bf16[1024]{0:T(1024)(128)(2,1)}) fusion(bf16[16,1024]{1,0:T(8,128)(2,1)} %get-tuple-element.26), kind=kLoop, calls=%fused_computation | loop fusion | bytes 8192 | tf_op jit(solution)/shard_map/slice | solution.py:660

commit v6 on v5

--- a/solution.py
+++ b/solution.py
@@ -67,12 +67,6 @@
 
     at_core = (dp, y * CORES + (1 - core))
     colours = ((0, y, at_y, x, at_x), (1, x, at_x, y, at_y))
-
-    barrier = pltpu.get_barrier_semaphore()
-    peers = [at_z(d) for d in range(1, nz)] + [at_x(d) for d in range(1, NX)]
-    peers = peers + [at_y(d) for d in range(1, ny)] + [at_core]
-    for peer in peers:
-        pl.semaphore_signal(barrier, inc=1, device_id=peer, device_id_type=pl.DeviceIdType.MESH)
 
     top = 0
     for src in (one, two, three, lin, small):
@@ -110,7 +104,6 @@
         return (colour * CORES + 1 - core) * half
 
     order = list(range(1, fan)) + [0]
-    pl.semaphore_wait(barrier, len(peers))
     core_copies = []
     for d in order:
         for colour, first, _, _, _ in colours:
@@ -237,37 +230,23 @@
             top += dst.shape[0]
 
 
-def sum_everywhere(pieces, nz, ny):
+def sum_scratch(nz):
     total = 2 * CORES * NX * NX * PIECE
     copies = 2 * (2 * (NX + 2 * (NX - 1)) + nz - 1)
-    vmem = pl.BlockSpec(memory_space=pltpu.VMEM)
-    packed = pl.pallas_call(
-        functools.partial(sum_kernel, nz, ny),
-        out_shape=jax.ShapeDtypeStruct((total, LANES), BF),
-        in_specs=[vmem] * len(pieces),
-        out_specs=vmem,
-        scratch_shapes=[
-            pltpu.VMEM((total, LANES), F32),
-            pltpu.VMEM((total, LANES), BF),
-            pltpu.VMEM((total, LANES), BF),
-            pltpu.VMEM((total // CORES, LANES), BF),
-            pltpu.VMEM((2, NX - 1, NX * PIECE, LANES), BF),
-            pltpu.VMEM((2, NX - 1, PIECE, LANES), BF),
-            pltpu.VMEM((nz, SUB, LANES), F32),
-            pltpu.VMEM((nz, SUB, LANES), BF),
-            pltpu.VMEM((nz - 1, SUB, LANES), BF),
-            pltpu.VMEM((nz, SUB, LANES), BF),
-            pltpu.SemaphoreType.DMA((copies,)),
-            pltpu.SemaphoreType.DMA((copies,)),
-        ],
-        compiler_params=pltpu.CompilerParams(collective_id=0, has_side_effects=True),
-    )(*pieces)
-    return pl.pallas_call(
-        unpack_kernel,
-        out_shape=[jax.ShapeDtypeStruct(p.shape, BF) for p in pieces],
-        in_specs=[vmem],
-        out_specs=[vmem] * len(pieces),
-    )(packed)
+    return [
+        pltpu.VMEM((total, LANES), F32),
+        pltpu.VMEM((total, LANES), BF),
+        pltpu.VMEM((total, LANES), BF),
+        pltpu.VMEM((total // CORES, LANES), BF),
+        pltpu.VMEM((2, NX - 1, NX * PIECE, LANES), BF),
+        pltpu.VMEM((2, NX - 1, PIECE, LANES), BF),
+        pltpu.VMEM((nz, SUB, LANES), F32),
+        pltpu.VMEM((nz, SUB, LANES), BF),
+        pltpu.VMEM((nz - 1, SUB, LANES), BF),
+        pltpu.VMEM((nz, SUB, LANES), BF),
+        pltpu.SemaphoreType.DMA((copies,)),
+        pltpu.SemaphoreType.DMA((copies,)),
+    ]
 
 
 ROWS = 336
@@ -279,7 +258,7 @@
 
 
 def work_kernel(
-    tm_n, half, block_rows, scale, blocks, mel_ref, cot_ref, proj, conv_one, w_two, w_three, lin, gain, bias, taps,
+    tm_n, half, block_rows, scale, nz, blocks, mel_ref, cot_ref, proj, conv_one, w_two, w_three, lin, gain, bias, taps,
     one, two, three, g_lin, small,
     full, w_one, xw, up_snd, up_rcv, down_rcv, z1, z2, z3, a1, a2, a3, n_ref, inv_ref, u_ref, du_ref,
     eg_ref, gated_ref, em, dh_ref, sums, own_sem, send_sem, recv_sem,
@@ -301,7 +280,8 @@
 
     at_z = ((depth + 1 - 2 * (depth % 2)) * NX + x, tm)
     barrier = pltpu.get_barrier_semaphore()
-    peers = [at(d) for d in range(1, tm_n)] + [at_x(d) for d in range(1, NX)] + [at_z]
+    peers = [at(d) for d in range(1, tm_n)] + [at_x(d) for d in range(1, NX)]
+    peers = peers + [(((depth + d) % nz) * NX + x, tm) for d in range(1, nz)]
     for peer in peers:
         pl.semaphore_signal(barrier, inc=1, device_id=peer, device_id_type=pl.DeviceIdType.MESH)
 
@@ -569,7 +549,14 @@
         copy.wait_send()
 
 
-def work(operands, tm_n, half, block_rows, scale):
+def step_kernel(tm_n, half, block_rows, scale, nz, work_count, *refs):
+    ins, result, grads = refs[:11], refs[11], refs[12:17]
+    work_refs, sum_refs = refs[17 : 17 + work_count], refs[17 + work_count :]
+    work_kernel(tm_n, half, block_rows, scale, nz, *ins, *grads, *work_refs)
+    sum_kernel(nz, tm_n // CORES, *grads, result, *sum_refs)
+
+
+def work(operands, tm_n, half, block_rows, scale, nz):
     proj, lin = operands[3], operands[7]
     width = lin.shape[1]
     vmem = pl.BlockSpec(memory_space=pltpu.VMEM)
@@ -579,44 +566,50 @@
     def buf(*shape, dtype=BF):
         return pltpu.VMEM(shape, dtype)
 
-    return pl.pallas_call(
-        functools.partial(work_kernel, tm_n, half, block_rows, scale),
-        out_shape=[
-            jax.ShapeDtypeStruct(shape, F32)
-            for shape in ((240, 256), (768, 256), (768, 256), (256, width), (16, width))
-        ],
+    shapes = ((240, 256), (768, 256), (768, 256), (256, width), (16, width))
+    scratch = [
+        buf(tm_n, *proj.shape),
+        buf(768, 1024),
+        buf(ROWS, 768),
+        buf(RIM, 640),
+        buf(RIM, 640),
+        buf(RIM, 640),
+        buf(ROWS, 1024, dtype=F32),
+        buf(ROWS, 512, dtype=F32),
+        buf(ROWS, 256, dtype=F32),
+        buf(ROWS, 1024),
+        buf(ROWS, 512),
+        buf(ROWS, 256),
+        buf(ROWS, width, dtype=F32),
+        buf(ROWS, 128, dtype=F32),
+        buf(ROWS, width),
+        buf(ROWS, width, dtype=F32),
+        buf(ROWS, width),
+        buf(ROWS, width, dtype=F32),
+        buf(tm_n, ROWS, 256),
+        buf(ROWS, width),
+        buf(8, width, dtype=F32),
+        pltpu.SemaphoreType.DMA,
+        pltpu.SemaphoreType.DMA((copies,)),
+        pltpu.SemaphoreType.DMA((copies,)),
+    ]
+    grads = [buf(*shape, dtype=F32) for shape in shapes]
+    packed = pl.pallas_call(
+        functools.partial(step_kernel, tm_n, half, block_rows, scale, nz, len(scratch)),
+        out_shape=jax.ShapeDtypeStruct((2 * CORES * NX * NX * PIECE, LANES), BF),
         in_specs=[pl.BlockSpec(memory_space=pltpu.SMEM)] + [vmem] * 10,
-        out_specs=[vmem] * 5,
-        scratch_shapes=[
-            buf(tm_n, *proj.shape),
-            buf(768, 1024),
-            buf(ROWS, 768),
-            buf(RIM, 640),
-            buf(RIM, 640),
-            buf(RIM, 640),
-            buf(ROWS, 1024, dtype=F32),
-            buf(ROWS, 512, dtype=F32),
-            buf(ROWS, 256, dtype=F32),
-            buf(ROWS, 1024),
-            buf(ROWS, 512),
-            buf(ROWS, 256),
-            buf(ROWS, width, dtype=F32),
-            buf(ROWS, 128, dtype=F32),
-            buf(ROWS, width),
-            buf(ROWS, width, dtype=F32),
-            buf(ROWS, width),
-            buf(ROWS, width, dtype=F32),
-            buf(tm_n, ROWS, 256),
-            buf(ROWS, width),
-            buf(8, width, dtype=F32),
-            pltpu.SemaphoreType.DMA,
-            pltpu.SemaphoreType.DMA((copies,)),
-            pltpu.SemaphoreType.DMA((copies,)),
-        ],
+        out_specs=vmem,
+        scratch_shapes=grads + scratch + sum_scratch(nz),
         compiler_params=pltpu.CompilerParams(
-            collective_id=1, has_side_effects=True, vmem_limit_bytes=56 * 1024 * 1024
+            collective_id=0, has_side_effects=True, vmem_limit_bytes=56 * 1024 * 1024
         ),
     )(*operands)
+    return pl.pallas_call(
+        unpack_kernel,
+        out_shape=[jax.ShapeDtypeStruct(shape, BF) for shape in shapes],
+        in_specs=[vmem],
+        out_specs=[vmem] * len(shapes),
+    )(packed)
 
 
 def per_device(
@@ -637,7 +630,7 @@
     block_rows = mel.shape[1] // dp_count
     taps = dw_kernel.shape[0]
     total_rows = (dp_count * dp_count + 2) // 3 * block_rows * tm_count
-    results = work(
+    one, two, three, lin, small = work(
         (
             blocks,
             mel,
@@ -655,8 +648,8 @@
         taps // 2,
         block_rows,
         total_rows**-0.5,
+        dp_count // NX,
     )
-    one, two, three, lin, small = sum_everywhere(results, dp_count // NX, tm_count // CORES)
     return (one, two, three, lin, small[taps], small[taps + 1], small[:taps])
 
 

time: 101 us -> 95.6 us (0.947)
  Pallas kernels: 99.1 us -> 93.3 us
    pallas_call x3 -> x2, Pallas kernels: 99.1 us -> 93.3 us  [the longest x1 90.1 us: work(): pl.pallas_call(functools.partial(step_kernel, tm_n, half, block_rows, sca...]
where the time goes in v6:
time: 95.6 us; the launch traced here: 95.3 us
  Pallas kernels  93.3 us (98%)
  local copies, waits for them, and re-layouts  1.4 us (1%)
    pallas_call x1, Pallas kernels, work(): pl.pallas_call(functools.partial(step_kernel, tm_n, half, block_rows, sca...  90.1 us
    pallas_call x1, Pallas kernels, work(): pl.pallas_call(unpack_kernel, out_shape=[jax.ShapeDtypeStruct(shape, BF)...  3.17 us

profile of v6, /device:TPU:1, one launch (start us, length us, event | category | flops | bytes accessed | tf_op | source)
XLA Modules:
  0.0 95.3 jit_solution(15586673673757122658)
XLA Ops:
  0.6 90.1 %shard_map.162.packed = bf16[3072,256]{1,0:T(8,128)(2,1)} custom-call(s32[64]{0:T(128)} %refs_0_.1, bf16[1,320,640]{2,1,0:T(8,128)(2,1)} %refs_1_.1, bf16[1,320,1024]{2,1,0:T(8,128)(2,1)} %refs_2_.1, bf16[1024,256]{1,0:T(8,128)(2,1)} %refs_3_.1, bf16[240,256]{1,0:T(8,128)(2,1)} %refs_4_.1, bf16[768,256]{1,0:T(8,128)(2,1)} %refs_5_.1, ...), custom_call_target="tpu_custom_call" | custom-call | tf_op jit(solution)/shard_map/pallas_call | solution.py:597
  90.8 3.2 %shard_map.163 = (bf16[240,256]{1,0:T(8,128)(2,1)}, bf16[768,256]{1,0:T(8,128)(2,1)}, bf16[768,256]{1,0:T(8,128)(2,1)}, bf16[256,1024]{1,0:T(8,128)(2,1)}, bf16[16,1024]{1,0:T(8,128)(2,1)}) custom-call(bf16[3072,256]{1,0:T(8,128)(2,1)} %shard_map.162.packed), custom_call_target="tpu_custom_call" | custom-call | tf_op jit(solution)/shard_map/pallas_call | solution.py:607
  93.9 1.4 %slice_reduce_fusion = (bf16[1024]{0:T(1024)(128)(2,1)}, bf16[1024]{0:T(1024)(128)(2,1)}) fusion(bf16[16,1024]{1,0:T(8,128)(2,1)} %get-tuple-element.16), kind=kLoop, calls=%fused_computation | loop fusion | bytes 8192 | tf_op jit(solution)/shard_map/slice | solution.py:653
